TPU v7x, 128 devices: a whole 4x4x4 slice. The times are simulated.
128 devices in a mesh: row: 8 (over x_lo, z), col: 16 (over x_hi, y, core).
Axes of the slice: x: 4 (x_hi: 2, x_lo: 2; x = x_hi * 2 + x_lo), y: 4, z: 4, core: 2. Of those that a mesh axis runs over, the one named last changes fastest.
Arguments:
- amplitudes: float32 [16384, 16384], P('row', 'col'), may hold values from -1 to 1, as said below
- factors: float32 [16384, 256], P('row', 'col'), may hold values from -1.5 to 1.5
- occ_index: int32 [16384], replicated, may hold values from 0 to 63
- vir_index: int32 [16384], replicated, may hold values from 0 to 2047
- occ_energy: float32 [64], replicated, may hold values from -3 to -0.5
- vir_energy: float32 [2048], replicated, may hold values from 0.2 to 3
Outputs:
- new_amplitudes: float32 [16384, 16384], P('row', 'col')
Inputs may be any that keep to these rules, and one draw needn't show every extreme that they name: amplitudes is symmetric: amplitudes[p, q] equals amplitudes[q, p].
All inputs are finite; a program needn't handle non-finite values.
Results may differ from a plain program's by a relative error of at most 0.000096.
Values sent between devices are 32-bit elements; how exact they have to be, the bound alone decides.
A program may use at most 64 MiB of HBM per device.

v0:
```python
import jax
import jax.numpy as jnp
from jax import lax
from jax.sharding import PartitionSpec as P


def joined_along(tiles, dim):
    tiles = jnp.moveaxis(tiles, 0, dim)
    dims = tiles.shape
    return tiles.reshape(*dims[:dim], dims[dim] * dims[dim + 1], *dims[dim + 2 :])


def copy_for_each(array, axis):
    copies = jnp.broadcast_to(array, (lax.axis_size(axis), *array.shape))
    return lax.all_to_all(copies, axis, split_axis=0, concat_axis=0, tiled=True)


def collect(array, axis, dim):
    return joined_along(copy_for_each(array, axis), dim)


def cut_along(array, dim, size):
    before, after = (array.shape[:dim], array.shape[dim + 1 :])
    return jnp.moveaxis(array.reshape(*before, size, -1, *after), dim, 0)


def summed_on_arrival(array, axis, dim):
    size = lax.axis_size(axis)
    tiles = lax.all_to_all(cut_along(array, dim, size), axis, 0, 0, tiled=True)
    return jnp.sum(tiles, axis=0)


def pair_energy(occupied, virtual, occ_energy, vir_energy):
    occ_table = jnp.arange(occ_energy.shape[0], dtype=jnp.int32)
    vir_table = jnp.arange(vir_energy.shape[0], dtype=jnp.int32)
    picked_vir = jnp.sum(
        jnp.where(virtual[:, None] == vir_table[None, :], vir_energy[None, :], 0.0), axis=1
    )
    picked_occ = jnp.sum(
        jnp.where(occupied[:, None] == occ_table[None, :], occ_energy[None, :], 0.0), axis=1
    )
    return picked_vir - picked_occ


def local(amplitudes, factors, occ_index, vir_index, occ_energy, vir_energy):
    tile_rows = amplitudes.shape[0]
    tile_cols = amplitudes.shape[1]
    row_index = lax.axis_index("row")
    col_index = lax.axis_index("col")
    col_count = lax.axis_size("col")
    block_ratio = col_count // lax.axis_size("row")
    column_piece = collect(factors, "col", 1)
    contracted = lax.dot_general(
        amplitudes,
        column_piece,
        (((0,), (0,)), ((), ())),
        precision=lax.Precision.HIGHEST,
        preferred_element_type=jnp.float32,
    )
    joined = jnp.concatenate([column_piece, contracted], axis=0)
    row_factors = joined[:tile_rows]
    partial_sum = joined[tile_rows:]
    owned_block = lax.dynamic_slice_in_dim(
        row_factors, col_index % block_ratio * tile_cols, tile_cols, 0
    )
    owner_flag = jnp.where(row_index == col_index // block_ratio, 1.0, 0.0).astype(jnp.float32)
    partial_sum = partial_sum + owner_flag * owned_block
    column_share = summed_on_arrival(partial_sum, "row", 1)
    wide_col = collect(column_share, "row", 1)
    piece_rows = tile_cols // col_count
    split_block = wide_col.reshape(col_count, piece_rows, wide_col.shape[1])
    arrived = lax.all_to_all(split_block, "col", split_axis=0, concat_axis=0, tiled=True)
    needed = lax.dynamic_slice_in_dim(arrived, row_index * block_ratio, block_ratio, 0)
    whole_pieces = collect(needed, "col", 1)
    wide_row = whole_pieces.reshape(block_ratio * tile_cols, wide_col.shape[1])
    energy_rows = pair_energy(
        lax.dynamic_slice_in_dim(occ_index, row_index * tile_rows, tile_rows),
        lax.dynamic_slice_in_dim(vir_index, row_index * tile_rows, tile_rows),
        occ_energy,
        vir_energy,
    )
    energy_cols = pair_energy(
        lax.dynamic_slice_in_dim(occ_index, col_index * tile_cols, tile_cols),
        lax.dynamic_slice_in_dim(vir_index, col_index * tile_cols, tile_cols),
        occ_energy,
        vir_energy,
    )
    outer_sum = lax.dot_general(
        wide_row,
        wide_col,
        (((1,), (1,)), ((), ())),
        precision=lax.Precision.HIGHEST,
        preferred_element_type=jnp.float32,
    )
    return -outer_sum / (energy_rows[:, None] + energy_cols[None, :])


def solution(mesh):
    return jax.shard_map(
        local,
        mesh=mesh,
        in_specs=(P("row", "col"), P("row", "col"), P(), P(), P(), P()),
        out_specs=P("row", "col"),
        check_vma=False,
    )
```

profile of v0, /device:TPU:1, one launch (start us, length us, event | category | flops | bytes accessed | tf_op | source)
XLA Modules:
  0.0 160.3 jit_solution(1079546019210219984)
XLA Ops:
  0.0 2.5 %broadcast_in_dim.71 = f32[16,2048,16]{1,2,0:T(8,128)} broadcast(f32[2048,16]{0,1:T(8,128)} %param.7), dimensions={1,2} | broadcast | bytes 2228224 | tf_op jit(solution)/shard_map/broadcast_in_dim | solution.py:14
  2.5 8.4 %all-to-all-start = ((f32[16,2048,16]{1,2,0:T(8,128)}), f32[16,2048,16]{1,2,0:T(8,128)S(1)}, u32[]{:S(2)}, u32[]{:S(2)}) async-start(f32[16,2048,16]{1,2,0:T(8,128)} %broadcast_in_dim.71), calls=%async_computation | async-start | bytes 4194304 | tf_op jit(solution)/shard_map/all_to_all | solution.py:15
  10.9 28.3 %all-to-all-done = f32[16,2048,16]{1,2,0:T(8,128)S(1)} async-done(((f32[16,2048,16]{1,2,0:T(8,128)}), f32[16,2048,16]{1,2,0:T(8,128)S(1)}, u32[]{:S(2)}, u32[]{:S(2)}) %all-to-all-start) | async-done | bytes 2097184 | tf_op jit(solution)/shard_map/all_to_all | solution.py:15
  39.2 10.1 %convolution_add_fusion = f32[1024,256]{0,1:T(8,128)S(1)} fusion(f32[2048,1024]{1,0:T(8,128)} %param.6, f32[2048,256]{0,1:T(8,128)S(1)} %bitcast.18, s32[]{:T(128)S(6)} %select_n.48, f32[]{:T(128)S(6)} %select_n.46), kind=kOutput, calls=%fused_computation.5 | convolution fusion | flops 6442975232 | bytes 12582920 | tf_op jit(solution)/shard_map/dot_general | solution.py:53
  49.4 19.2 %all_to_all.25 = f32[8,1024,32]{1,2,0:T(8,128)S(1)} all-to-all(f32[8,1024,32]{1,2,0:T(8,128)S(1)} %bitcast.19), channel_id=1, replica_groups=mesh['row'=8,'col'=16] {'row'}, dimensions={0} | all-to-all | bytes 2097152 | tf_op jit(solution)/shard_map/all_to_all | solution.py:29
  68.6 0.1 reduce_sum.45
  68.6 0.1 broadcast_in_dim.72
  68.7 0.0 copy-start
  68.8 0.0 copy-start.1
  68.8 16.1 %all_to_all.26 = f32[8,1024,32]{1,2,0:T(8,128)S(1)} all-to-all(f32[8,1024,32]{1,2,0:T(8,128)S(1)} %broadcast_in_dim.72), channel_id=1, replica_groups=mesh['row'=8,'col'=16] {'row'}, dimensions={0} | all-to-all | bytes 2097152 | tf_op jit(solution)/shard_map/all_to_all | solution.py:15
  84.9 0.6 reshape_reshape.6
  85.5 2.0 %copy.10 = f32[16,64,256]{2,1,0:T(8,128)} copy(f32[16,64,256]{1,0,2:T(8,128)S(1)} %reshape_reshape.6) | data formatting | bytes 2097152 | tf_op jit(solution)/shard_map/reshape;reshape | solution.py:71
  87.5 11.4 %all-to-all-start.3 = ((f32[16,64,256]{2,1,0:T(8,128)}), f32[16,64,256]{2,1,0:T(8,128)S(1)}, u32[]{:S(2)}, u32[]{:S(2)}) async-start(f32[16,64,256]{2,1,0:T(8,128)} %copy.10), calls=%async_computation.3 | async-start | bytes 2097152 | tf_op jit(solution)/shard_map/all_to_all | solution.py:72
  98.9 17.1 %all-to-all-done.3 = f32[16,64,256]{2,1,0:T(8,128)S(1)} async-done(((f32[16,64,256]{2,1,0:T(8,128)}), f32[16,64,256]{2,1,0:T(8,128)S(1)}, u32[]{:S(2)}, u32[]{:S(2)}) %all-to-all-start.3) | async-done | bytes 1048608 | tf_op jit(solution)/shard_map/all_to_all | solution.py:72
  116.0 1.6 broadcast_in_dim.73
  117.5 4.5 %all-to-all-start.4 = ((f32[16,2,64,256]{3,2,1,0:T(8,128)}), f32[16,2,64,256]{3,2,1,0:T(8,128)S(1)}, u32[]{:S(2)}, u32[]{:S(2)}) async-start(f32[16,2,64,256]{3,2,1,0:T(8,128)} %broadcast_in_dim.73), calls=%async_computation.4 | async-start | bytes 4194304 | tf_op jit(solution)/shard_map/all_to_all | solution.py:15
  122.0 0.7 dynamic_slice.23
  122.7 0.7 dynamic_slice.22
  123.4 0.7 dynamic_slice.21
  124.1 0.7 dynamic_slice.20
  124.8 0.0 copy-done
  124.8 0.1 select_reduce_fusion.3
  124.9 0.0 copy-done.1
  124.9 1.2 select_reduce_fusion.1
  126.1 0.2 select_reduce_fusion.2
  126.3 2.3 %select_reduce_fusion = f32[2048]{0:T(1024)S(1)} fusion(f32[2048]{0:T(1024)S(1)} %copy-done.1, s32[2048]{0:T(1024)S(1)} %dynamic_slice.20), kind=kLoop, calls=%fused_computation | loop fusion | flops 12580864 | bytes 24576 | tf_op jit(solution)/shard_map/reduce_sum | solution.py:36
  128.6 21.9 %all-to-all-done.4 = f32[16,2,64,256]{3,2,1,0:T(8,128)S(1)} async-done(((f32[16,2,64,256]{3,2,1,0:T(8,128)}), f32[16,2,64,256]{3,2,1,0:T(8,128)S(1)}, u32[]{:S(2)}, u32[]{:S(2)}) %all-to-all-start.4) | async-done | bytes 2097184 | tf_op jit(solution)/shard_map/all_to_all | solution.py:15
  150.5 0.1 copy.11
  150.6 9.7 %add_divide_fusion = f32[2048,1024]{1,0:T(8,128)} fusion(f32[2048,256]{1,0:T(8,128)S(1)} %bitcast.22, f32[1024,256]{0,1:T(8,128)S(1)} %bitcast.21, f32[1024]{0:T(1024)S(1)} %sub.20, f32[2048]{0:T(1024)S(1)} %sub.19), kind=kOutput, calls=%fused_computation.2 | convolution fusion | flops 6448742400 | bytes 11546624 | tf_op jit(solution)/shard_map/dot_general | solution.py:88
  (3 shorter events, 0.0 us)
Async XLA Ops:
  2.5 36.8 %all-to-all-start = ((f32[16,2048,16]{1,2,0:T(8,128)}), f32[16,2048,16]{1,2,0:T(8,128)S(1)}, u32[]{:S(2)}, u32[]{:S(2)}) async-start(f32[16,2048,16]{1,2,0:T(8,128)} %broadcast_in_dim.71), calls=%async_computation | async-start | bytes 4194304 | tf_op jit(solution)/shard_map/all_to_all | solution.py:15
  68.7 56.1 %copy-start = (f32[64]{0:T(128)S(1)}, f32[64]{0:T(128)}, u32[]{:S(2)}) copy-start(f32[64]{0:T(128)} %param.10) | copy-start | bytes 772
  68.8 56.2 %copy-start.1 = (f32[2048]{0:T(1024)S(1)}, f32[2048]{0:T(1024)}, u32[]{:S(2)}) copy-start(f32[2048]{0:T(1024)} %param.11) | copy-start | bytes 24580
  87.5 28.5 %all-to-all-start.3 = ((f32[16,64,256]{2,1,0:T(8,128)}), f32[16,64,256]{2,1,0:T(8,128)S(1)}, u32[]{:S(2)}, u32[]{:S(2)}) async-start(f32[16,64,256]{2,1,0:T(8,128)} %copy.10), calls=%async_computation.3 | async-start | bytes 2097152 | tf_op jit(solution)/shard_map/all_to_all | solution.py:72
  117.5 33.0 %all-to-all-start.4 = ((f32[16,2,64,256]{3,2,1,0:T(8,128)}), f32[16,2,64,256]{3,2,1,0:T(8,128)S(1)}, u32[]{:S(2)}, u32[]{:S(2)}) async-start(f32[16,2,64,256]{3,2,1,0:T(8,128)} %broadcast_in_dim.73), calls=%async_computation.4 | async-start | bytes 4194304 | tf_op jit(solution)/shard_map/all_to_all | solution.py:15
where the time goes:
time: 161 us; the launch traced here: 160 us
  waiting for transfers between devices  67.3 us (42%)
  blocking collectives  35.3 us (22%)
  starting transfers between devices  24.4 us (15%)
  matrix products  19.8 us (12%)
  local copies, waits for them, and re-layouts  9.6 us (6%)
  other arithmetic  3.8 us (2%)
    all_to_all x2, waiting for transfers between devices, copy_for_each(): return lax.all_to_all(copies, axis, split_axis=0, concat_axis=0, tiled=True)  50.2 us
    all_to_all x1, blocking collectives, summed_on_arrival(): tiles = lax.all_to_all(cut_along(array, dim, size), axis, 0, 0, tiled=True)  19.2 us
    all_to_all x1, waiting for transfers between devices, local(): lax.all_to_all(split_block, 'col', split_axis=0, concat_axis=0, tiled=True)  17.1 us
    all_to_all x1, blocking collectives, copy_for_each(): return lax.all_to_all(copies, axis, split_axis=0, concat_axis=0, tiled=True)  16.1 us
    all_to_all x2, starting transfers between devices, copy_for_each(): return lax.all_to_all(copies, axis, split_axis=0, concat_axis=0, tiled=True)  13 us
    all_to_all x1, starting transfers between devices, local(): lax.all_to_all(split_block, 'col', split_axis=0, concat_axis=0, tiled=True)  11.4 us
    dot_general x1, matrix products, local(): lax.dot_general(amplitudes, column_piece, (((0,), (0,)), ((), ())), preci...  10.1 us
    dot_general x1, matrix products, local(): lax.dot_general(wide_row, wide_col, (((1,), (1,)), ((), ())), precision=l...  9.7 us
  transfers between devices with their start and end apart: 3, of which 3 were waited for; matrix products, arithmetic and copies ran while one was open for 4% of the time, Pallas kernels for 0%

commit v1 on v0

v1 whole, which is shorter than its diff:
```python
import functools

import jax
import jax.numpy as jnp
from jax import lax
from jax.experimental import pallas as pl
from jax.experimental.pallas import tpu as pltpu
from jax.sharding import PartitionSpec as P

MESH = pl.DeviceIdType.MESH
F32 = jnp.float32
BF16 = jnp.bfloat16
RING = ("pA", "mB", "pB", "mA", "fA", "fB")
NAMES = []
for t_ in range(2):
    for r_ in ("f0", "c0", "c1", "r0", "r1"):
        NAMES += [f"{r_}{t_}{m_}" for m_ in RING]
    NAMES += [f"s{q_}{j_}{t_}" for q_ in ("f", "r") for j_ in ("0", "m", "p", "2")]
    NAMES += [f"{m_}{t_}" for m_ in ("s1p", "s1m", "s2pA", "s2pB", "s2mA", "s2mB", "s3", "cx", "sw")]
    NAMES += [f"{m_}{t_}" for m_ in ("rxA", "rxB", "rrA", "rrB", "sr0x", "srmx", "srpx", "sr2x")]
NAMES += ["fxA", "fxB", "frA", "frB"]
ID = {n_: i_ for i_, n_ in enumerate(NAMES)}


def split(v):
    hi = v.astype(BF16)
    return hi, (v - hi.astype(F32)).astype(BF16)


def exchange_kernel(
    a_hbm, f_hbm, dr_hbm, dc_hbm,
    abuf, ah, al, ft, fhl, rlp, rlm, pt, r1a, r1b, r2p, r2m, sx, r3, dc, dn, dr, qlp, qlm,
    ssem, rsem, asem, lsem,
):
    row, col = lax.axis_index("row"), lax.axis_index("col")
    x_lo, z = row // 4, row % 4
    s = col // 2
    x_hi, y, core = s // 4, s % 4, col % 2
    x = 2 * x_hi + x_lo

    def dev(xh, xl, yy, zz, cc):
        return (xl * 4 + zz, xh * 8 + yy * 2 + cc)

    yp, ym, y2 = (y + 1) % 4, (y + 3) % 4, (y + 2) % 4
    zp, zm, z2 = (z + 1) % 4, (z + 3) % 4, (z + 2) % 4
    xp, xm = (x + 1) % 4, (x + 3) % 4
    d_yp, d_ym = dev(x_hi, x_lo, yp, z, core), dev(x_hi, x_lo, ym, z, core)
    d_zp, d_zm = dev(x_hi, x_lo, y, zp, core), dev(x_hi, x_lo, y, zm, core)
    d_xp, d_xm = dev(xp // 2, xp % 2, y, z, core), dev(xm // 2, xm % 2, y, z, core)
    d_xn = dev(x_hi, 1 - x_lo, y, z, core)
    d_sib = dev(x_hi, x_lo, y, z, 1 - core)
    d_tr = dev(x_lo, x_hi, z, y, core)
    diag = row == s
    off_diag = row != s

    sends = {}

    def make(name, src, dst, to):
        i = ID[name]
        return pltpu.make_async_remote_copy(
            src_ref=src, dst_ref=dst, send_sem=ssem.at[i], recv_sem=rsem.at[i],
            device_id=to, device_id_type=MESH)

    def start(name, src, dst, to):
        sends[name] = make(name, src, dst, to)
        sends[name].start()

    def recv(name, ref):
        make(name, ref, ref, d_sib).wait_recv()

    class Ring:
        def __init__(self, name, slot, pos, up, down, half):
            self.n, self.slot, self.up, self.down, self.half = name, slot, up, down, half
            self.p, self.u, self.d, self.o = pos, (pos + 1) % 4, (pos + 3) % 4, (pos + 2) % 4

        def part(self, ref, which):
            return ref.at[pl.ds(which * self.half, self.half)]

        def own(self, src=None):
            dst = self.slot(self.p)
            src = dst if src is None else src
            for m, w, to in (("pA", 0, self.up), ("mB", 1, self.down), ("pB", 1, self.up), ("mA", 0, self.down)):
                start(self.n + m, self.part(src, w), self.part(dst, w), to)

        def fwd(self):
            ref = self.part(self.slot(self.d), 0)
            recv(self.n + "pA", ref)
            start(self.n + "fA", ref, ref, self.up)
            ref = self.part(self.slot(self.u), 1)
            recv(self.n + "mB", ref)
            start(self.n + "fB", ref, ref, self.down)

        def near(self):
            recv(self.n + "pB", self.part(self.slot(self.d), 1))
            recv(self.n + "mA", self.part(self.slot(self.u), 0))

        def far(self):
            recv(self.n + "fA", self.part(self.slot(self.o), 0))
            recv(self.n + "fB", self.part(self.slot(self.o), 1))

    def a_copy(i):
        rows = pl.ds(i * 256, 256)
        return pltpu.make_async_copy(a_hbm.at[rows], abuf.at[rows], asem.at[i])

    for i in range(8):
        a_copy(i).start()
    own_f = pltpu.make_async_copy(f_hbm, ft.at[x_hi, y, core], lsem.at[0])
    own_f.start()

    barrier = pltpu.get_barrier_semaphore()
    for d in (d_yp, d_ym, d_zp, d_zm, d_xp, d_xm, d_sib):
        pl.semaphore_signal(barrier, inc=1, device_id=d, device_id_type=MESH)

    @pl.when(off_diag)
    def _():
        pl.semaphore_signal(barrier, inc=1, device_id=d_tr, device_id_type=MESH)
        pl.semaphore_wait(barrier, 8)

    @pl.when(diag)
    def _():
        pl.semaphore_wait(barrier, 7)

    def f_slot(h):
        return lambda i: ft.at[h, i, core]

    fr = [Ring(f"f0{t}", f_slot(x_hi if t == 0 else 1 - x_hi), y, d_yp, d_ym, 8) for t in range(2)]
    lo8, hi8 = pl.ds(0, 8), pl.ds(8, 8)
    start("fxA", f_hbm.at[lo8], rlp, d_xp)
    start("fxB", f_hbm.at[hi8], rlm, d_xm)
    fr[0].own(f_hbm)
    sib_f0 = ft.at[x_hi, y, core]
    start("sf00", f_hbm, sib_f0, d_sib)

    def split_a(lo, hi):
        def body(i, carry):
            a_copy(i).wait()
            rows = pl.ds(pl.multiple_of(i * 256, 256), 256)
            for xl in range(2):
                for zz in range(4):
                    r = xl * 4 + zz
                    h, l = split(abuf[rows, r * 128:(r + 1) * 128])
                    ah[zz, rows, xl * 128:(xl + 1) * 128] = h
                    al[zz, rows, xl * 128:(xl + 1) * 128] = l
            return carry
        lax.fori_loop(lo, hi, body, 0)

    def f_sib(t, j, pos):
        h = x_hi if t == 0 else 1 - x_hi
        start(f"sf{j}{t}", ft.at[h, pos, core], ft.at[h, pos, core], d_sib)

    def f_sib_recv(t):
        h = x_hi if t == 0 else 1 - x_hi
        for j, pos in (("0", y), ("m", ym), ("p", yp), ("2", y2)):
            recv(f"sf{j}{t}", ft.at[h, pos, 1 - core])

    split_a(0, 4)
    recv("fxA", rlp)
    start("frA", rlp, ft.at[1 - xp // 2, y, core, lo8], d_xp)
    recv("fxB", rlm)
    start("frB", rlm, ft.at[1 - xm // 2, y, core, hi8], d_xm)
    split_a(4, 6)
    fr[0].fwd()
    fr[0].near()
    f_sib(0, "m", ym)
    f_sib(0, "p", yp)
    split_a(6, 8)
    recv("frA", ft.at[1 - x_hi, y, core, lo8])
    recv("frB", ft.at[1 - x_hi, y, core, hi8])
    fr[1].own()
    f_sib(1, "0", y)
    fr[0].far()
    f_sib(0, "2", y2)
    own_f.wait()
    f_sib_recv(0)

    def split_f(t):
        h = x_hi if t == 0 else 1 - x_hi
        hi, lo = split(ft[h].reshape(128, 2048))
        fhl[0:128] = hi
        fhl[128:256] = lo

    def product(t, zz):
        h = x_hi if t == 0 else 1 - x_hi
        both = jnp.dot(fhl[...], ah[zz], preferred_element_type=F32)
        low = jnp.dot(fhl[0:128], al[zz], preferred_element_type=F32)
        p = both[:128] + (both[128:] + low)
        for xl in range(2):
            pt[t, zz, xl] = p[:, xl * 128:(xl + 1) * 128]

        @pl.when(diag)
        def _():
            for xl in range(2):
                at = pl.multiple_of(core * 1024 + (xl * 4 + zz) * 128, 128)
                pt[t, zz, xl] += ft[h, :, :, :, pl.ds(at, 128)].reshape(128, 128)

    up, dn_ = pl.ds(0, 64), pl.ds(64, 64)

    def reduce_first(t):
        start(f"s1p{t}", pt.at[t, z2, :, up], r1a.at[t], d_zp)
        start(f"s1m{t}", pt.at[t, z2, :, dn_], r1b.at[t], d_zm)

    def reduce_near(t, j):
        if j == "p":
            start(f"s2pB{t}", pt.at[t, zp, :, dn_], r2p.at[t, :, dn_], d_zp)
        else:
            start(f"s2mA{t}", pt.at[t, zm, :, up], r2m.at[t, :, up], d_zm)

    def reduce_relay(t):
        recv(f"s1p{t}", r1a.at[t])
        pt[t, zp, :, 0:64] += r1a[t]
        start(f"s2pA{t}", pt.at[t, zp, :, up], r2p.at[t, :, up], d_zp)
        recv(f"s1m{t}", r1b.at[t])
        pt[t, zm, :, 64:128] += r1b[t]
        start(f"s2mB{t}", pt.at[t, zm, :, dn_], r2m.at[t, :, dn_], d_zm)

    def reduce_cross(t):
        recv(f"s2pB{t}", r2p.at[t, :, dn_])
        recv(f"s2mA{t}", r2m.at[t, :, up])
        recv(f"s2pA{t}", r2p.at[t, :, up])
        recv(f"s2mB{t}", r2m.at[t, :, dn_])
        o = 1 - x_lo
        sx[t] = pt[t, z, o] + r2p[t, o] + r2m[t, o]
        start(f"s3{t}", sx.at[t], r3.at[t], d_xn)

    def kc(t):
        return x_hi if t == 0 else 1 - x_hi

    def kr(t):
        return x_lo if t == 0 else 1 - x_lo

    def c_ring(t, j):
        xl = x_lo if j == 0 else 1 - x_lo
        return Ring(f"c{j}{t}", lambda i: dc.at[kc(t), xl * 4 + i], z, d_zp, d_zm, 64)

    def r_ring(t, j):
        xh = x_hi if j == 0 else 1 - x_hi
        return Ring(f"r{j}{t}", lambda i: dr.at[kr(t), core, xh * 4 + i], y, d_yp, d_ym, 64)

    cr = [[c_ring(t, j) for j in range(2)] for t in range(2)]
    rr = [[r_ring(t, j) for j in range(2)] for t in range(2)]

    def dressed(t):
        own = pt[t, z, x_lo] + r2p[t, x_lo] + r2m[t, x_lo]
        recv(f"s3{t}", r3.at[t])
        d = own + r3[t]
        dc[kc(t), row] = d
        dt = d.T

        @pl.when(off_diag)
        def _():
            dn[t] = dt
            make(f"sw{t}", dn.at[t], dr.at[kc(t), core, row], d_tr).start()

        @pl.when(diag)
        def _():
            dr[kc(t), core, row] = dt

        start(f"cx{t}", dc.at[kc(t), row], dc.at[kc(t), row], d_xn)
        cr[t][0].own()

    def swap_in(t):
        @pl.when(off_diag)
        def _():
            recv(f"sw{t}", dr.at[kr(t), core, s])

        mine = dr.at[kr(t), core, s]
        start(f"rxA{t}", mine.at[up], qlp.at[t], d_xp)
        start(f"rxB{t}", mine.at[dn_], qlm.at[t], d_xm)
        rr[t][0].own()
        start(f"sr0{t}", mine, mine, d_sib)

    def c_other(t):
        recv(f"cx{t}", dc.at[kc(t), (1 - x_lo) * 4 + z])
        cr[t][1].own()

    def r_relay(t):
        k = 1 - kr(t)
        recv(f"rxA{t}", qlp.at[t])
        start(f"rrA{t}", qlp.at[t], dr.at[k, core, (1 - xp // 2) * 4 + y, up], d_xp)
        recv(f"rxB{t}", qlm.at[t])
        start(f"rrB{t}", qlm.at[t], dr.at[k, core, (1 - xm // 2) * 4 + y, dn_], d_xm)

    def r_sib(t, j, tag, pos):
        xh = x_hi if j == 0 else 1 - x_hi
        ref = dr.at[kr(t), core, xh * 4 + pos]
        start(f"sr{tag}{t}" if j == 0 else f"sr{tag}x{t}", ref, ref, d_sib)

    def r_other(t):
        o = (1 - x_hi) * 4 + y
        recv(f"rrA{t}", dr.at[kr(t), core, o, up])
        recv(f"rrB{t}", dr.at[kr(t), core, o, dn_])
        rr[t][1].own()
        r_sib(t, 1, "0", y)

    def r_near(t, j):
        rr[t][j].near()
        r_sib(t, j, "m", ym)
        r_sib(t, j, "p", yp)

    def r_far(t, j):
        rr[t][j].far()
        r_sib(t, j, "2", y2)

    def r_sib_recv(t):
        for j in range(2):
            xh = x_hi if j == 0 else 1 - x_hi
            for tag, pos in (("0", y), ("m", ym), ("p", yp), ("2", y2)):
                recv(f"sr{tag}{t}" if j == 0 else f"sr{tag}x{t}", dr.at[kr(t), 1 - core, xh * 4 + pos])

    split_f(0)
    product(0, z2)
    reduce_first(0)
    product(0, zp)
    reduce_near(0, "p")
    product(0, zm)
    reduce_near(0, "m")
    fr[1].fwd()
    fr[1].near()
    f_sib(1, "m", ym)
    f_sib(1, "p", yp)
    reduce_relay(0)
    product(0, z)
    fr[1].far()
    f_sib(1, "2", y2)
    reduce_cross(0)
    f_sib_recv(1)
    split_f(1)
    product(1, z2)
    reduce_first(1)
    dressed(0)
    product(1, zp)
    reduce_near(1, "p")
    product(1, zm)
    reduce_near(1, "m")
    swap_in(0)
    reduce_relay(1)
    product(1, z)
    r_relay(0)
    c_other(0)
    cr[0][0].fwd()
    rr[0][0].fwd()
    r_other(0)
    r_near(0, 0)
    reduce_cross(1)
    cr[0][1].fwd()
    rr[0][1].fwd()
    dressed(1)
    cr[0][0].near()
    r_far(0, 0)
    r_near(0, 1)
    cr[0][0].far()
    cr[0][1].near()
    r_far(0, 1)
    cr[0][1].far()
    swap_in(1)
    r_sib_recv(0)
    outs = [
        pltpu.make_async_copy(dr.at[kr(0)], dr_hbm.at[kr(0)], lsem.at[1]),
        pltpu.make_async_copy(dc.at[kc(0)], dc_hbm.at[kc(0)], lsem.at[2]),
    ]
    for o in outs:
        o.start()
    c_other(1)
    r_relay(1)
    cr[1][0].fwd()
    rr[1][0].fwd()
    r_other(1)
    r_near(1, 0)
    cr[1][1].fwd()
    rr[1][1].fwd()
    cr[1][0].near()
    cr[1][0].far()
    r_far(1, 0)
    r_near(1, 1)
    cr[1][1].near()
    cr[1][1].far()
    last = pltpu.make_async_copy(dc.at[kc(1)], dc_hbm.at[kc(1)], lsem.at[3])
    last.start()
    r_far(1, 1)
    r_sib_recv(1)
    final = pltpu.make_async_copy(dr.at[kr(1)], dr_hbm.at[kr(1)], lsem.at[4])
    final.start()
    for c in sends.values():
        c.wait_send()

    @pl.when(off_diag)
    def _():
        for t in range(2):
            make(f"sw{t}", dn.at[t], dr.at[kc(t), core, row], d_tr).wait_send()

    for o in outs + [last, final]:
        o.wait()


def outer_kernel(dr_ref, dc_ref, occ_ref, vir_ref, eocc_ref, evir_ref, out_ref, ch, cl, ecol, erow):
    @pl.when(pl.program_id(0) == 0)
    def _():
        for k in range(2):
            for r in range(8):
                h, l = split(dc_ref[k, r])
                ch[k * 128:(k + 1) * 128, r * 128:(r + 1) * 128] = h
                cl[k * 128:(k + 1) * 128, r * 128:(r + 1) * 128] = l
        row, col = lax.axis_index("row"), lax.axis_index("col")
        occ_rows, vir_rows = [], []
        for start, size in ((row * 16, 16), (col * 8, 8)):
            at = pl.ds(pl.multiple_of(start, 8), size)
            occ_rows.append(occ_ref[at])
            vir_rows.append(vir_ref[at])
        occ = jnp.concatenate(occ_rows, axis=0)
        vir = jnp.concatenate(vir_rows, axis=0)
        low, high = vir & 127, vir >> 7
        picked = jnp.zeros((24, 128), F32)
        for h in range(16):
            table = jnp.broadcast_to(evir_ref[h:h + 1], (24, 128))
            got = jnp.take_along_axis(table, low, axis=1, mode="promise_in_bounds")
            picked = jnp.where(high == h, got, picked)
        taken = jnp.zeros((24, 128), F32)
        for o in range(64):
            taken = jnp.where(occ == o, eocc_ref[o], taken)
        negative = taken - picked
        erow[...] = negative[16:24]
        for i in range(16):
            ecol[i * 128:(i + 1) * 128] = jnp.broadcast_to(negative[i:i + 1], (128, 128)).T

    x = jnp.concatenate([dr_ref[0], dr_ref[1]], axis=1)
    h, l = split(x)
    acc = jnp.dot(h, ch[...], preferred_element_type=F32)
    acc += jnp.dot(l, ch[...], preferred_element_type=F32)
    acc += jnp.dot(h, cl[...], preferred_element_type=F32)
    rows = pl.ds(pl.multiple_of(pl.program_id(0) * 256, 256), 256)
    e = ecol[rows]
    for n in range(8):
        lanes = slice(n * 128, (n + 1) * 128)
        out_ref[:, lanes] = acc[:, lanes] / (e + erow[n:n + 1])


def local(amplitudes, factors, occ_index, vir_index, occ_energy, vir_energy):
    hbm = pl.BlockSpec(memory_space=pl.ANY)
    vmem = lambda *shape: pltpu.VMEM(shape, F32)
    dr, dc = pl.pallas_call(
        exchange_kernel,
        out_shape=(
            jax.ShapeDtypeStruct((2, 2, 8, 128, 128), F32),
            jax.ShapeDtypeStruct((2, 8, 128, 128), F32),
        ),
        in_specs=[hbm, hbm],
        out_specs=(hbm, hbm),
        scratch_shapes=[
            vmem(2048, 1024),
            pltpu.VMEM((4, 2048, 256), BF16),
            pltpu.VMEM((4, 2048, 256), BF16),
            vmem(2, 4, 2, 16, 2048),
            pltpu.VMEM((256, 2048), BF16),
            vmem(8, 2048),
            vmem(8, 2048),
            vmem(2, 4, 2, 128, 128),
            vmem(2, 2, 64, 128),
            vmem(2, 2, 64, 128),
            vmem(2, 2, 128, 128),
            vmem(2, 2, 128, 128),
            vmem(2, 128, 128),
            vmem(2, 128, 128),
            vmem(2, 8, 128, 128),
            vmem(2, 128, 128),
            vmem(2, 2, 8, 128, 128),
            vmem(2, 64, 128),
            vmem(2, 64, 128),
            pltpu.SemaphoreType.DMA((len(NAMES),)),
            pltpu.SemaphoreType.DMA((len(NAMES),)),
            pltpu.SemaphoreType.DMA((8,)),
            pltpu.SemaphoreType.DMA((5,)),
        ],
        compiler_params=pltpu.CompilerParams(
            collective_id=0, has_side_effects=True, vmem_limit_bytes=48 * 1024 * 1024),
        name="exchange",
    )(amplitudes, factors.T)
    whole = lambda *shape: pl.BlockSpec(shape, lambda i: (0,) * len(shape))
    return pl.pallas_call(
        outer_kernel,
        grid=(8,),
        out_shape=jax.ShapeDtypeStruct((2048, 1024), F32),
        in_specs=[
            pl.BlockSpec((2, 256, 128), lambda i: (0, i, 0)),
            whole(2, 8, 128, 128),
            whole(128, 128),
            whole(128, 128),
            pl.BlockSpec(memory_space=pltpu.SMEM),
            whole(16, 128),
        ],
        out_specs=pl.BlockSpec((256, 1024), lambda i: (i, 0)),
        scratch_shapes=[
            pltpu.VMEM((256, 1024), BF16),
            pltpu.VMEM((256, 1024), BF16),
            vmem(2048, 128),
            vmem(8, 128),
        ],
        compiler_params=pltpu.CompilerParams(vmem_limit_bytes=32 * 1024 * 1024),
        name="outer",
    )(
        dr.reshape(2, 2048, 128), dc, occ_index.reshape(128, 128), vir_index.reshape(128, 128),
        occ_energy, vir_energy.reshape(16, 128),
    )


def solution(mesh):
    return jax.shard_map(
        local,
        mesh=mesh,
        in_specs=(P("row", "col"), P("row", "col"), P(), P(), P(), P()),
        out_specs=P("row", "col"),
        check_vma=False,
    )
```

time: 161 us -> 75.7 us (0.47)
  Pallas kernels: 0 us -> 74.6 us
  waiting for transfers between devices: 67.3 us -> 0 us
  blocking collectives: 35.3 us -> 0 us
  starting transfers between devices: 24.4 us -> 0 us
  matrix products: 19.8 us -> 0 us
  local copies, waits for them, and re-layouts: 9.6 us -> 0.93 us
  other arithmetic: 3.8 us -> 0 us
    pallas_call x0 -> x2, Pallas kernels: none -> 74.6 us  [the longest x1 66.4 us: local(): pl.pallas_call(exchange_kernel, out_shape=(jax.ShapeDtypeStruct((2, 2, 8,...]
    all_to_all x3 -> x0, waiting for transfers between devices: 67.3 us -> none  [the longest x2 50.2 us: copy_for_each(): return lax.all_to_all(copies, axis, split_axis=0, concat_axis=0, tiled=True)]
    all_to_all x2 -> x0, blocking collectives: 35.3 us -> none  [the longest x1 19.2 us: summed_on_arrival(): tiles = lax.all_to_all(cut_along(array, dim, size), axis, 0, 0, tiled=True)]
    all_to_all x3 -> x0, starting transfers between devices: 24.4 us -> none  [the longest x2 13 us: copy_for_each(): return lax.all_to_all(copies, axis, split_axis=0, concat_axis=0, tiled=True)]
    dot_general x2 -> x0, matrix products: 19.8 us -> none  [the longest x1 10.1 us: local(): lax.dot_general(amplitudes, column_piece, (((0,), (0,)), ((), ())), preci...]
    broadcast_in_dim x3 -> x0, local copies, waits for them, and re-layouts: 4.12 us -> none  [copy_for_each(): copies = jnp.broadcast_to(array, (lax.axis_size(axis), *array.shape))]
    reduce_sum x5 -> x0, other arithmetic: 3.79 us -> none  [the longest x2 3.47 us: pair_energy(): jnp.sum(jnp.where(virtual[:, None] == vir_table[None, :], vir_energy[None...]
    dynamic_slice x5 -> x0, local copies, waits for them, and re-layouts: 2.78 us -> none  [the longest x1 0.7 us: local(): lax.dynamic_slice_in_dim(occ_index, row_index * tile_rows, tile_rows)]
  transfers between devices with their start and end apart: 3 -> 0, of which waited for: 3 -> 0; matrix products, arithmetic and copies ran while one was open for 4% -> 0% of each run, Pallas kernels for 0% -> 0%
where the time goes in v1:
time: 75.7 us; the launch traced here: 75.6 us
  Pallas kernels  74.6 us (99%)
  local copies, waits for them, and re-layouts  0.93 us (1%)
    pallas_call x1, Pallas kernels, local(): pl.pallas_call(exchange_kernel, out_shape=(jax.ShapeDtypeStruct((2, 2, 8,...  66.4 us
    pallas_call x1, Pallas kernels, local(): pl.pallas_call(outer_kernel, grid=(8,), out_shape=jax.ShapeDtypeStruct((2...  8.19 us

profile of v1, /device:TPU:1, one launch (start us, length us, event | category | flops | bytes accessed | tf_op | source)
XLA Modules:
  0.0 75.6 jit_solution(4847341628958672093)
XLA Ops:
  0.0 0.0 copy-start.4
  0.0 0.0 copy-start
  0.0 0.9 %copy-done = f32[2048,16]{0,1:T(8,128)S(1)} copy-done((f32[2048,16]{0,1:T(8,128)S(1)}, f32[2048,16]{0,1:T(8,128)}, u32[]{:S(2)}) %copy-start) | copy-done | bytes 131096
  0.9 0.0 copy-start.1
  0.9 0.0 copy-start.2
  0.9 0.0 copy-start.3
  0.9 66.4 %exchange.1 = (f32[2,2,8,128,128]{4,3,2,1,0:T(8,128)S(1)}, f32[2,8,128,128]{3,2,1,0:T(8,128)S(1)}) custom-call(f32[2048,1024]{1,0:T(8,128)} %a_hbm.1, f32[16,2048]{1,0:T(8,128)S(1)} %bitcast.6), custom_call_target="tpu_custom_call" | custom-call | tf_op jit(solution)/shard_map/exchange/pallas_call | solution.py:440
  67.4 0.0 copy-done.4
  67.4 0.0 copy-done.1
  67.4 0.0 copy-done.2
  67.4 0.0 copy-done.3
  67.4 8.2 %outer.1 = f32[2048,1024]{1,0:T(8,128)} custom-call(f32[2,2048,128]{2,1,0:T(8,128)S(1)} %bitcast.5, f32[2,8,128,128]{3,2,1,0:T(8,128)S(1)} %get-tuple-element.8.dc_ref, s32[128,128]{1,0:T(8,128)S(1)} %bitcast.7, s32[128,128]{1,0:T(8,128)S(1)} %bitcast.8, f32[64]{0:T(128)S(1)} %copy-done.4, f32[16,128]{1,0:T(8,128)S(1)} %bitcast.9), custom_call_target="tpu_custom_call" | custom-call | tf_op jit(solution)/shard_map/outer/pallas_call | solution.py:478
Async XLA Ops:
  0.0 67.4 %copy-start.4 = (f32[64]{0:T(128)S(1)}, f32[64]{0:T(128)}, u32[]{:S(2)}) copy-start(f32[64]{0:T(128)} %eocc_ref.1) | copy-start | bytes 772
  0.0 0.9 %copy-start = (f32[2048,16]{0,1:T(8,128)S(1)}, f32[2048,16]{0,1:T(8,128)}, u32[]{:S(2)}) copy-start(f32[2048,16]{0,1:T(8,128)} %param.7) | copy-start | bytes 393220
  0.9 66.5 %copy-start.1 = (s32[16384]{0:T(1024)S(1)}, s32[16384]{0:T(1024)}, u32[]{:S(2)}) copy-start(s32[16384]{0:T(1024)} %param.8) | copy-start | bytes 196612
  0.9 66.5 %copy-start.2 = (s32[16384]{0:T(1024)S(1)}, s32[16384]{0:T(1024)}, u32[]{:S(2)}) copy-start(s32[16384]{0:T(1024)} %param.9) | copy-start | bytes 196612
  0.9 66.5 %copy-start.3 = (f32[2048]{0:T(1024)S(1)}, f32[2048]{0:T(1024)}, u32[]{:S(2)}) copy-start(f32[2048]{0:T(1024)} %param.11) | copy-start | bytes 24580

commit v2 on v0

v2 whole, which is shorter than its diff:
```python
import functools

import jax
import jax.numpy as jnp
from jax import lax
from jax.experimental import pallas as pl
from jax.experimental.pallas import tpu as pltpu
from jax.sharding import PartitionSpec as P

MESH = pl.DeviceIdType.MESH
F32 = jnp.float32
BF16 = jnp.bfloat16
RING = ("pA", "mB", "pB", "mA", "fA", "fB")
NAMES = ["fx"]
for t_ in range(2):
    for r_ in ("f0", "f1"):
        NAMES += [f"{r_}{m_}" for m_ in RING if t_ == 0]
    for r_ in ("c0", "c1", "r0", "r1"):
        NAMES += [f"{r_}{t_}{m_}" for m_ in RING]
    NAMES += [f"{q_}{t_}{j_}" for q_ in ("sf", "sr", "sq") for j_ in ("0", "m", "p", "2")]
    NAMES += [f"{m_}{t_}" for m_ in ("s1p", "s1m", "s2pA", "s2pB", "s2mA", "s2mB", "s3", "cx", "sw", "sx")]
ID = {n_: i_ for i_, n_ in enumerate(NAMES)}

ORDER = (
    "f0.own", "spA0", "spA1", "spA2", "spA3", "f0.fA", "f0.fB", "f0.nm", "f0.np", "f1.own", "f0.far", "spF0",
    "mm0.2", "mm0.p", "f1.fA", "f1.fB", "mm0.m", "mm0.0", "f1.nm", "f1.np", "rl0p", "rl0m", "f1.far", "spF1",
    "mm1.2", "mm1.p", "mm1.m", "mm1.0", "cr0", "rl1p", "rl1m", "c00.own", "cr1", "c00.fA", "c10.own", "c00.fB",
    "c00.nm", "c00.np", "r00.own", "c01.own", "r10.own", "c10.fB", "c10.fA", "c10.np", "r00.fA", "r00.fB",
    "c10.nm", "c00.far", "r00.nm", "r00.np", "c11.own", "c01.fA", "c01.fB", "r10.fA", "r10.fB", "c01.nm",
    "c01.np", "r10.nm", "r10.np", "c10.far", "r01.own", "r00.far", "c11.fA", "c11.fB", "r11.own", "c11.nm",
    "c11.np", "r10.far", "c01.far", "rf0", "r01.fA", "r01.fB", "c11.far", "r01.nm", "r01.np", "r11.fA",
    "r11.fB", "r11.nm", "r11.np", "r01.far", "r11.far", "rf1",
)


def split(v):
    hi = v.astype(BF16)
    return hi, (v - hi.astype(F32)).astype(BF16)


def exchange_kernel(
    a_hbm, f_hbm, dr, dc,
    abuf, ah, al, ft, fhl, pt, r1a, r1b, r2p, r2m, sx, r3, dp, dn,
    ssem, rsem, asem, lsem, msem,
):
    row, col = lax.axis_index("row"), lax.axis_index("col")
    x_lo, z = row // 4, row % 4
    s = col // 2
    x_hi, y, core = s // 4, s % 4, col % 2

    def dev(xh, xl, yy, zz, cc):
        return (xl * 4 + zz, xh * 8 + yy * 2 + cc)

    yp, ym, y2 = (y + 1) % 4, (y + 3) % 4, (y + 2) % 4
    zp, zm, z2 = (z + 1) % 4, (z + 3) % 4, (z + 2) % 4
    d_yp, d_ym = dev(x_hi, x_lo, yp, z, core), dev(x_hi, x_lo, ym, z, core)
    d_zp, d_zm = dev(x_hi, x_lo, y, zp, core), dev(x_hi, x_lo, y, zm, core)
    d_x2 = dev(1 - x_hi, x_lo, y, z, core)
    d_xn = dev(x_hi, 1 - x_lo, y, z, core)
    d_sib = dev(x_hi, x_lo, y, z, 1 - core)
    d_tr = dev(x_lo, x_hi, z, y, core)
    d_tx = dev(1 - x_lo, x_hi, z, y, core)
    d_from_tx = dev(x_lo, 1 - x_hi, z, y, core)
    diag = row == s
    off_diag = row != s

    sends, got = {}, set()

    def make(name, src, dst, to):
        i = ID[name]
        return pltpu.make_async_remote_copy(
            src_ref=src, dst_ref=dst, send_sem=ssem.at[i], recv_sem=rsem.at[i],
            device_id=to, device_id_type=MESH)

    def start(name, src, dst, to):
        sends[name] = make(name, src, dst, to)
        sends[name].start()

    def recv(name, ref):
        if name not in got:
            got.add(name)
            make(name, ref, ref, d_sib).wait_recv()

    steps = {}

    def step(name):
        def keep(f):
            steps[name] = f
        return keep

    def ring(n, slot, pos, to_up, to_down, half, own, sib=None):
        u, d, o = (pos + 1) % 4, (pos + 3) % 4, (pos + 2) % 4

        def part(i, which):
            return slot(i).at[pl.ds(which * half, half)]

        def to_sib(tag, i):
            if sib is not None:
                start(sib + tag, slot(i), slot(i), d_sib)

        def send_own(src=None):
            src = slot(pos) if src is None else src
            for m, w, to in (("pA", 0, to_up), ("mB", 1, to_down), ("pB", 1, to_up), ("mA", 0, to_down)):
                start(n + m, src.at[pl.ds(w * half, half)], part(pos, w), to)
            if sib is not None:
                start(sib + "0", src, slot(pos), d_sib)

        @step(n + ".own")
        def _():
            own(send_own)

        @step(n + ".fA")
        def _():
            recv(n + "pA", part(d, 0))
            start(n + "fA", part(d, 0), part(d, 0), to_up)

        @step(n + ".fB")
        def _():
            recv(n + "mB", part(u, 1))
            start(n + "fB", part(u, 1), part(u, 1), to_down)

        @step(n + ".nm")
        def _():
            recv(n + "pA", part(d, 0))
            recv(n + "pB", part(d, 1))
            to_sib("m", d)

        @step(n + ".np")
        def _():
            recv(n + "mA", part(u, 0))
            recv(n + "mB", part(u, 1))
            to_sib("p", u)

        @step(n + ".far")
        def _():
            recv(n + "fA", part(o, 0))
            recv(n + "fB", part(o, 1))
            to_sib("2", o)

    def a_copy(i):
        rows = pl.ds(i * 256, 256)
        return pltpu.make_async_copy(a_hbm.at[rows], abuf.at[rows], asem.at[i])

    for i in range(8):
        a_copy(i).start()
    own_f = pltpu.make_async_copy(f_hbm, ft.at[x_hi, y, core], lsem.at[0])
    own_f.start()

    barrier = pltpu.get_barrier_semaphore()
    for d in (d_yp, d_ym, d_zp, d_zm, d_x2, d_xn, d_sib, d_from_tx):
        pl.semaphore_signal(barrier, inc=1, device_id=d, device_id_type=MESH)

    @pl.when(off_diag)
    def _():
        pl.semaphore_signal(barrier, inc=1, device_id=d_tr, device_id_type=MESH)
        pl.semaphore_wait(barrier, 9)

    @pl.when(diag)
    def _():
        pl.semaphore_wait(barrier, 8)

    def kf(t):
        return x_hi if t == 0 else 1 - x_hi

    def kr(t):
        return x_lo if t == 0 else 1 - x_lo

    def own_f0(send):
        start("fx", f_hbm, ft.at[x_hi, y, core], d_x2)
        send(f_hbm)

    def own_f1(send):
        recv("fx", ft.at[1 - x_hi, y, core])
        send()

    for t, own in enumerate((own_f0, own_f1)):
        ring(f"f{t}", lambda i, t=t: ft.at[kf(t), i, core], y, d_yp, d_ym, 8, own, f"sf{t}")

    for q in range(4):
        @step(f"spA{q}")
        def _(q=q):
            def body(i, carry):
                a_copy(i).wait()
                rows = pl.ds(pl.multiple_of(i * 256, 256), 256)
                for xl in range(2):
                    for zz in range(4):
                        r = xl * 4 + zz
                        h, l = split(abuf[rows, r * 128:(r + 1) * 128])
                        ah[zz, rows, xl * 128:(xl + 1) * 128] = h
                        al[zz, rows, xl * 128:(xl + 1) * 128] = l
                return carry
            lax.fori_loop(2 * q, 2 * q + 2, body, 0)

    up, down = pl.ds(0, 64), pl.ds(64, 64)

    def product(t, zz):
        h = kf(t)
        both = jnp.dot(fhl[...], ah[zz], preferred_element_type=F32)
        low = jnp.dot(fhl[0:128], al[zz], preferred_element_type=F32)
        p = both[:128] + (both[128:] + low)
        for xl in range(2):
            pt[t, zz, xl] = p[:, xl * 128:(xl + 1) * 128]

        @pl.when(diag)
        def _():
            for xl in range(2):
                at = pl.multiple_of(core * 1024 + (xl * 4 + zz) * 128, 128)
                pt[t, zz, xl] += ft[h, :, :, :, pl.ds(at, 128)].reshape(128, 128)

    for t in range(2):
        @step(f"spF{t}")
        def _(t=t):
            if t == 0:
                own_f.wait()
            for j, pos in (("0", y), ("m", ym), ("p", yp), ("2", y2)):
                recv(f"sf{t}{j}", ft.at[kf(t), pos, 1 - core])
            hi, lo = split(ft[kf(t)].reshape(128, 2048))
            fhl[0:128] = hi
            fhl[128:256] = lo

        @step(f"mm{t}.2")
        def _(t=t):
            product(t, z2)
            start(f"s1p{t}", pt.at[t, z2, :, up], r1a.at[t], d_zp)
            start(f"s1m{t}", pt.at[t, z2, :, down], r1b.at[t], d_zm)

        @step(f"mm{t}.p")
        def _(t=t):
            product(t, zp)
            start(f"s2pB{t}", pt.at[t, zp, :, down], r2p.at[t, :, down], d_zp)

        @step(f"mm{t}.m")
        def _(t=t):
            product(t, zm)
            start(f"s2mA{t}", pt.at[t, zm, :, up], r2m.at[t, :, up], d_zm)

        @step(f"mm{t}.0")
        def _(t=t):
            product(t, z)

        @step(f"rl{t}p")
        def _(t=t):
            recv(f"s1p{t}", r1a.at[t])
            pt[t, zp, :, 0:64] += r1a[t]
            start(f"s2pA{t}", pt.at[t, zp, :, up], r2p.at[t, :, up], d_zp)

        @step(f"rl{t}m")
        def _(t=t):
            recv(f"s1m{t}", r1b.at[t])
            pt[t, zm, :, 64:128] += r1b[t]
            start(f"s2mB{t}", pt.at[t, zm, :, down], r2m.at[t, :, down], d_zm)

        @step(f"cr{t}")
        def _(t=t):
            recv(f"s2pA{t}", r2p.at[t, :, up])
            recv(f"s2pB{t}", r2p.at[t, :, down])
            recv(f"s2mA{t}", r2m.at[t, :, up])
            recv(f"s2mB{t}", r2m.at[t, :, down])
            o = 1 - x_lo
            sx[t] = pt[t, z, o] + r2p[t, o] + r2m[t, o]
            start(f"s3{t}", sx.at[t], r3.at[t], d_xn)

        def own_c0(send, t=t):
            own = pt[t, z, x_lo] + r2p[t, x_lo] + r2m[t, x_lo]
            recv(f"s3{t}", r3.at[t])
            d = own + r3[t]
            dn[t] = d.T
            start(f"sx{t}", dn.at[t], dr.at[kf(t), core, row], d_tx)

            @pl.when(off_diag)
            def _():
                make(f"sw{t}", dn.at[t], dr.at[kf(t), core, row], d_tr).start()

            @pl.when(diag)
            def _():
                pltpu.make_async_copy(dn.at[t], dr.at[kf(t), core, row], msem.at[t]).start()

            dp[t] = d
            start(f"cx{t}", dp.at[t], dc.at[kf(t), row], d_xn)
            send(dp.at[t])
            pltpu.make_async_copy(dp.at[t], dc.at[kf(t), row], lsem.at[1 + t]).start()

        def own_c1(send, t=t):
            recv(f"cx{t}", dc.at[kf(t), (1 - x_lo) * 4 + z])
            send()

        def own_r0(send, t=t):
            mine = dr.at[kr(t), core, s]

            @pl.when(off_diag)
            def _():
                make(f"sw{t}", mine, mine, d_sib).wait_recv()

            @pl.when(diag)
            def _():
                pltpu.make_async_copy(dn.at[t], mine, msem.at[t]).wait()

            send()

        def own_r1(send, t=t):
            recv(f"sx{t}", dr.at[kr(t), core, (1 - x_hi) * 4 + y])
            send()

        for j, own in enumerate((own_c0, own_c1)):
            xl = x_lo if j == 0 else 1 - x_lo
            ring(f"c{j}{t}", lambda i, t=t, xl=xl: dc.at[kf(t), xl * 4 + i], z, d_zp, d_zm, 64, own)
        for j, own in enumerate((own_r0, own_r1)):
            xh = x_hi if j == 0 else 1 - x_hi
            ring(f"r{j}{t}", lambda i, t=t, xh=xh: dr.at[kr(t), core, xh * 4 + i], y, d_yp, d_ym, 64, own,
                 f"{'sr' if j == 0 else 'sq'}{t}")

        @step(f"rf{t}")
        def _(t=t):
            for j in range(2):
                xh = x_hi if j == 0 else 1 - x_hi
                for tag, pos in (("0", y), ("m", ym), ("p", yp), ("2", y2)):
                    recv(f"{'sr' if j == 0 else 'sq'}{t}{tag}", dr.at[kr(t), 1 - core, xh * 4 + pos])

    for name in ORDER:
        steps[name]()

    for c in sends.values():
        c.wait_send()

    @pl.when(off_diag)
    def _():
        for t in range(2):
            make(f"sw{t}", dn.at[t], dr.at[kf(t), core, row], d_tr).wait_send()

    for t in range(2):
        pltpu.make_async_copy(dp.at[t], dc.at[kf(t), row], lsem.at[1 + t]).wait()


OUTER_ROWS = (128, 384, 512, 512, 512)


def outer_kernel(dr_ref, dc_ref, occ_ref, vir_ref, evir_ref, eocc_ref, out_hbm, ch, cl, ecol, erow, obuf, sem):
    for k in range(2):
        for r in range(8):
            h, l = split(dc_ref[k, r])
            ch[k * 128:(k + 1) * 128, r * 128:(r + 1) * 128] = h
            cl[k * 128:(k + 1) * 128, r * 128:(r + 1) * 128] = l
    row, col = lax.axis_index("row"), lax.axis_index("col")
    occ_rows, vir_rows = [], []
    for first, size in ((row * 16, 16), (col * 8, 8)):
        at = pl.ds(pl.multiple_of(first, 8), size)
        occ_rows.append(occ_ref[at])
        vir_rows.append(vir_ref[at])
    occ = jnp.concatenate(occ_rows, axis=0)
    vir = jnp.concatenate(vir_rows, axis=0)
    low, high = vir & 127, vir >> 7
    picked = jnp.zeros((24, 128), F32)
    for h in range(16):
        table = jnp.broadcast_to(evir_ref[h:h + 1], (24, 128))
        got = jnp.take_along_axis(table, low, axis=1, mode="promise_in_bounds")
        picked = jnp.where(high == h, got, picked)
    taken = jnp.zeros((24, 128), F32)
    for o in range(64):
        taken = jnp.where(occ == o, eocc_ref[o], taken)
    negative = taken - picked
    erow[...] = negative[16:24]
    for i in range(16):
        ecol[i * 128:(i + 1) * 128] = jnp.broadcast_to(negative[i:i + 1], (128, 128)).T

    copies = []
    first = 0
    for i, size in enumerate(OUTER_ROWS):
        rows = slice(first, first + size)
        x = jnp.concatenate([dr_ref[0, rows], dr_ref[1, rows]], axis=1)
        h, l = split(x)
        acc = jnp.dot(h, ch[...], preferred_element_type=F32)
        acc += jnp.dot(l, ch[...], preferred_element_type=F32)
        acc += jnp.dot(h, cl[...], preferred_element_type=F32)
        e = ecol[rows]
        for n in range(8):
            lanes = slice(n * 128, (n + 1) * 128)
            obuf[rows, lanes] = acc[:, lanes] / (e + erow[n:n + 1])
        copies.append(pltpu.make_async_copy(obuf.at[rows], out_hbm.at[rows], sem.at[i]))
        copies[-1].start()
        first += size
    for c in copies:
        c.wait()


def local(amplitudes, factors, occ_index, vir_index, occ_energy, vir_energy):
    hbm = pl.BlockSpec(memory_space=pl.ANY)
    vmem = lambda *shape: pltpu.VMEM(shape, F32)
    dr, dc = pl.pallas_call(
        exchange_kernel,
        out_shape=(
            jax.ShapeDtypeStruct((2, 2, 8, 128, 128), F32),
            jax.ShapeDtypeStruct((2, 8, 128, 128), F32),
        ),
        in_specs=[hbm, pl.BlockSpec(memory_space=pltpu.HBM)],
        out_specs=(hbm, hbm),
        scratch_shapes=[
            vmem(2048, 1024),
            pltpu.VMEM((4, 2048, 256), BF16),
            pltpu.VMEM((4, 2048, 256), BF16),
            vmem(2, 4, 2, 16, 2048),
            pltpu.VMEM((256, 2048), BF16),
            vmem(2, 4, 2, 128, 128),
            vmem(2, 2, 64, 128),
            vmem(2, 2, 64, 128),
            vmem(2, 2, 128, 128),
            vmem(2, 2, 128, 128),
            vmem(2, 128, 128),
            vmem(2, 128, 128),
            vmem(2, 128, 128),
            vmem(2, 128, 128),
            pltpu.SemaphoreType.DMA((len(NAMES),)),
            pltpu.SemaphoreType.DMA((len(NAMES),)),
            pltpu.SemaphoreType.DMA((8,)),
            pltpu.SemaphoreType.DMA((3,)),
            pltpu.SemaphoreType.DMA((2,)),
        ],
        compiler_params=pltpu.CompilerParams(
            collective_id=0, has_side_effects=True, vmem_limit_bytes=48 * 1024 * 1024),
        name="exchange",
    )(amplitudes, factors.T)
    in_vmem = pl.BlockSpec(memory_space=pltpu.VMEM)
    return pl.pallas_call(
        outer_kernel,
        out_shape=jax.ShapeDtypeStruct((2048, 1024), F32),
        in_specs=[in_vmem] * 5 + [pl.BlockSpec(memory_space=pltpu.SMEM)],
        out_specs=hbm,
        scratch_shapes=[
            pltpu.VMEM((256, 1024), BF16),
            pltpu.VMEM((256, 1024), BF16),
            vmem(2048, 128),
            vmem(8, 128),
            vmem(2048, 1024),
            pltpu.SemaphoreType.DMA((len(OUTER_ROWS),)),
        ],
        compiler_params=pltpu.CompilerParams(vmem_limit_bytes=32 * 1024 * 1024),
        name="outer",
    )(
        dr.reshape(2, 2048, 128), dc, occ_index.reshape(128, 128), vir_index.reshape(128, 128),
        vir_energy.reshape(16, 128), occ_energy,
    )


def solution(mesh):
    return jax.shard_map(
        local,
        mesh=mesh,
        in_specs=(P("row", "col"), P("row", "col"), P(), P(), P(), P()),
        out_specs=P("row", "col"),
        check_vma=False,
    )
```

time: 161 us -> 68.3 us (0.42)
  waiting for transfers between devices: 67.3 us -> 0 us
  Pallas kernels: 0 us -> 67.2 us
  blocking collectives: 35.3 us -> 0 us
  starting transfers between devices: 24.4 us -> 0 us
  matrix products: 19.8 us -> 0 us
  local copies, waits for them, and re-layouts: 9.6 us -> 0.93 us
  other arithmetic: 3.8 us -> 0 us
    all_to_all x3 -> x0, waiting for transfers between devices: 67.3 us -> none  [the longest x2 50.2 us: copy_for_each(): return lax.all_to_all(copies, axis, split_axis=0, concat_axis=0, tiled=True)]
    pallas_call x0 -> x2, Pallas kernels: none -> 67.2 us  [the longest x1 61.5 us: local(): pl.pallas_call(exchange_kernel, out_shape=(jax.ShapeDtypeStruct((2, 2, 8,...]
    all_to_all x2 -> x0, blocking collectives: 35.3 us -> none  [the longest x1 19.2 us: summed_on_arrival(): tiles = lax.all_to_all(cut_along(array, dim, size), axis, 0, 0, tiled=True)]
    all_to_all x3 -> x0, starting transfers between devices: 24.4 us -> none  [the longest x2 13 us: copy_for_each(): return lax.all_to_all(copies, axis, split_axis=0, concat_axis=0, tiled=True)]
    dot_general x2 -> x0, matrix products: 19.8 us -> none  [the longest x1 10.1 us: local(): lax.dot_general(amplitudes, column_piece, (((0,), (0,)), ((), ())), preci...]
    broadcast_in_dim x3 -> x0, local copies, waits for them, and re-layouts: 4.12 us -> none  [copy_for_each(): copies = jnp.broadcast_to(array, (lax.axis_size(axis), *array.shape))]
    reduce_sum x5 -> x0, other arithmetic: 3.79 us -> none  [the longest x2 3.47 us: pair_energy(): jnp.sum(jnp.where(virtual[:, None] == vir_table[None, :], vir_energy[None...]
    dynamic_slice x5 -> x0, local copies, waits for them, and re-layouts: 2.78 us -> none  [the longest x1 0.7 us: local(): lax.dynamic_slice_in_dim(occ_index, row_index * tile_rows, tile_rows)]
  transfers between devices with their start and end apart: 3 -> 0, of which waited for: 3 -> 0; matrix products, arithmetic and copies ran while one was open for 4% -> 0% of each run, Pallas kernels for 0% -> 0%
where the time goes in v2:
time: 68.3 us; the launch traced here: 68.2 us
  Pallas kernels  67.2 us (98%)
  local copies, waits for them, and re-layouts  0.93 us (1%)
    pallas_call x1, Pallas kernels, local(): pl.pallas_call(exchange_kernel, out_shape=(jax.ShapeDtypeStruct((2, 2, 8,...  61.5 us
    pallas_call x1, Pallas kernels, local(): pl.pallas_call(outer_kernel, out_shape=jax.ShapeDtypeStruct((2048, 1024),...  5.69 us

profile of v2, /device:TPU:1, one launch (start us, length us, event | category | flops | bytes accessed | tf_op | source)
XLA Modules:
  0.0 68.2 jit_solution(11549303059527909377)
XLA Ops:
  0.0 0.0 copy-start.4
  0.0 0.0 copy-start
  0.0 0.9 %copy-done = f32[2048,16]{0,1:T(8,128)S(1)} copy-done((f32[2048,16]{0,1:T(8,128)S(1)}, f32[2048,16]{0,1:T(8,128)}, u32[]{:S(2)}) %copy-start) | copy-done | bytes 131096
  0.9 0.0 copy-start.1
  0.9 0.0 copy-start.2
  0.9 0.0 copy-start.3
  0.9 61.5 %exchange.1 = (f32[2,2,8,128,128]{4,3,2,1,0:T(8,128)S(1)}, f32[2,8,128,128]{3,2,1,0:T(8,128)S(1)}) custom-call(f32[2048,1024]{1,0:T(8,128)} %a_hbm.1, f32[16,2048]{1,0:T(8,128)S(1)} %bitcast.6), custom_call_target="tpu_custom_call" | custom-call | tf_op jit(solution)/shard_map/exchange/pallas_call | solution.py:388
  62.4 0.0 copy-done.4
  62.4 0.0 copy-done.1
  62.5 0.0 copy-done.2
  62.5 0.0 copy-done.3
  62.5 5.7 %outer.1 = f32[2048,1024]{1,0:T(8,128)} custom-call(f32[2,2048,128]{2,1,0:T(8,128)S(1)} %bitcast.5, f32[2,8,128,128]{3,2,1,0:T(8,128)S(1)} %get-tuple-element.8.dc_ref, s32[128,128]{1,0:T(8,128)S(1)} %bitcast.7, s32[128,128]{1,0:T(8,128)S(1)} %bitcast.8, f32[16,128]{1,0:T(8,128)S(1)} %bitcast.9, f32[64]{0:T(128)S(1)} %copy-done.4), custom_call_target="tpu_custom_call" | custom-call | tf_op jit(solution)/shard_map/outer/pallas_call | solution.py:422
Async XLA Ops:
  0.0 62.4 %copy-start.4 = (f32[64]{0:T(128)S(1)}, f32[64]{0:T(128)}, u32[]{:S(2)}) copy-start(f32[64]{0:T(128)} %eocc_ref.1) | copy-start | bytes 772
  0.0 0.9 %copy-start = (f32[2048,16]{0,1:T(8,128)S(1)}, f32[2048,16]{0,1:T(8,128)}, u32[]{:S(2)}) copy-start(f32[2048,16]{0,1:T(8,128)} %param.7) | copy-start | bytes 393220
  0.9 61.5 %copy-start.1 = (s32[16384]{0:T(1024)S(1)}, s32[16384]{0:T(1024)}, u32[]{:S(2)}) copy-start(s32[16384]{0:T(1024)} %param.8) | copy-start | bytes 196612
  0.9 61.5 %copy-start.2 = (s32[16384]{0:T(1024)S(1)}, s32[16384]{0:T(1024)}, u32[]{:S(2)}) copy-start(s32[16384]{0:T(1024)} %param.9) | copy-start | bytes 196612
  0.9 61.5 %copy-start.3 = (f32[2048]{0:T(1024)S(1)}, f32[2048]{0:T(1024)}, u32[]{:S(2)}) copy-start(f32[2048]{0:T(1024)} %param.11) | copy-start | bytes 24580

commit v3 on v2

--- a/solution.py
+++ b/solution.py
@@ -24,12 +24,12 @@
 ORDER = (
     "f0.own", "spA0", "spA1", "spA2", "spA3", "f0.fA", "f0.fB", "f0.nm", "f0.np", "f1.own", "f0.far", "spF0",
     "mm0.2", "mm0.p", "f1.fA", "f1.fB", "mm0.m", "mm0.0", "f1.nm", "f1.np", "rl0p", "rl0m", "f1.far", "spF1",
-    "mm1.2", "mm1.p", "mm1.m", "mm1.0", "cr0", "rl1p", "rl1m", "c00.own", "cr1", "c00.fA", "c10.own", "c00.fB",
-    "c00.nm", "c00.np", "r00.own", "c01.own", "r10.own", "c10.fB", "c10.fA", "c10.np", "r00.fA", "r00.fB",
-    "c10.nm", "c00.far", "r00.nm", "r00.np", "c11.own", "c01.fA", "c01.fB", "r10.fA", "r10.fB", "c01.nm",
-    "c01.np", "r10.nm", "r10.np", "c10.far", "r01.own", "r00.far", "c11.fA", "c11.fB", "r11.own", "c11.nm",
-    "c11.np", "r10.far", "c01.far", "rf0", "r01.fA", "r01.fB", "c11.far", "r01.nm", "r01.np", "r11.fA",
-    "r11.fB", "r11.nm", "r11.np", "r01.far", "r11.far", "rf1",
+    "mm1.2", "mm1.p", "mm1.m", "mm1.0", "cr0", "rl1p", "rl1m", "c00.own", "cr1", "c10.own", "c00.fA", "c00.fB",
+    "c01.own", "r00.own", "c00.nm", "c00.np", "c10.fA", "c10.fB", "r10.own", "c10.nm", "c10.np", "c00.far",
+    "c11.own", "r00.fA", "r00.fB", "c01.fA", "c01.fB", "r00.nm", "r00.np", "c01.nm", "c01.np", "r01.own",
+    "r10.fA", "r10.fB", "c10.far", "r10.nm", "r10.np", "r11.own", "c11.fA", "c11.fB", "r00.far", "c11.nm",
+    "c11.np", "r01.fA", "r01.fB", "c01.far", "r01.nm", "r01.np", "c11.far", "r10.far", "r11.fA", "r11.fB",
+    "rf0", "r11.nm", "r11.np", "r01.far", "r11.far", "rf1",
 )
 
 
@@ -58,11 +58,13 @@
     d_x2 = dev(1 - x_hi, x_lo, y, z, core)
     d_xn = dev(x_hi, 1 - x_lo, y, z, core)
     d_sib = dev(x_hi, x_lo, y, z, 1 - core)
-    d_tr = dev(x_lo, x_hi, z, y, core)
-    d_tx = dev(1 - x_lo, x_hi, z, y, core)
-    d_from_tx = dev(x_lo, 1 - x_hi, z, y, core)
+    d_tr = dev(x_lo, x_hi, (y + z) % 4, y, core)
+    d_from_tr = dev(x_lo, x_hi, z, (y - z + 4) % 4, core)
+    d_tx = dev(1 - x_lo, x_hi, (y + z) % 4, y, core)
+    d_from_tx = dev(x_lo, 1 - x_hi, z, (y - z + 4) % 4, core)
+    stays = (x_hi == x_lo) & (y == 0) & (z == 0)
+    moves = jnp.logical_not(stays)
     diag = row == s
-    off_diag = row != s
 
     sends, got = {}, set()
 
@@ -150,12 +152,12 @@
     for d in (d_yp, d_ym, d_zp, d_zm, d_x2, d_xn, d_sib, d_from_tx):
         pl.semaphore_signal(barrier, inc=1, device_id=d, device_id_type=MESH)
 
-    @pl.when(off_diag)
+    @pl.when(moves)
     def _():
-        pl.semaphore_signal(barrier, inc=1, device_id=d_tr, device_id_type=MESH)
+        pl.semaphore_signal(barrier, inc=1, device_id=d_from_tr, device_id_type=MESH)
         pl.semaphore_wait(barrier, 9)
 
-    @pl.when(diag)
+    @pl.when(stays)
     def _():
         pl.semaphore_wait(barrier, 8)
 
@@ -267,11 +269,11 @@
             dn[t] = d.T
             start(f"sx{t}", dn.at[t], dr.at[kf(t), core, row], d_tx)
 
-            @pl.when(off_diag)
+            @pl.when(moves)
             def _():
                 make(f"sw{t}", dn.at[t], dr.at[kf(t), core, row], d_tr).start()
 
-            @pl.when(diag)
+            @pl.when(stays)
             def _():
                 pltpu.make_async_copy(dn.at[t], dr.at[kf(t), core, row], msem.at[t]).start()
 
@@ -285,20 +287,20 @@
             send()
 
         def own_r0(send, t=t):
-            mine = dr.at[kr(t), core, s]
-
-            @pl.when(off_diag)
+            mine = dr.at[kr(t), core, x_hi * 4 + (y - z + 4) % 4]
+
+            @pl.when(moves)
             def _():
                 make(f"sw{t}", mine, mine, d_sib).wait_recv()
 
-            @pl.when(diag)
+            @pl.when(stays)
             def _():
                 pltpu.make_async_copy(dn.at[t], mine, msem.at[t]).wait()
 
             send()
 
         def own_r1(send, t=t):
-            recv(f"sx{t}", dr.at[kr(t), core, (1 - x_hi) * 4 + y])
+            recv(f"sx{t}", dr.at[kr(t), core, (1 - x_hi) * 4 + (y - z + 4) % 4])
             send()
 
         for j, own in enumerate((own_c0, own_c1)):
@@ -306,7 +308,7 @@
             ring(f"c{j}{t}", lambda i, t=t, xl=xl: dc.at[kf(t), xl * 4 + i], z, d_zp, d_zm, 64, own)
         for j, own in enumerate((own_r0, own_r1)):
             xh = x_hi if j == 0 else 1 - x_hi
-            ring(f"r{j}{t}", lambda i, t=t, xh=xh: dr.at[kr(t), core, xh * 4 + i], y, d_yp, d_ym, 64, own,
+            ring(f"r{j}{t}", lambda i, t=t, xh=xh: dr.at[kr(t), core, xh * 4 + (i - z + 4) % 4], y, d_yp, d_ym, 64, own,
                  f"{'sr' if j == 0 else 'sq'}{t}")
 
         @step(f"rf{t}")
@@ -314,7 +316,7 @@
             for j in range(2):
                 xh = x_hi if j == 0 else 1 - x_hi
                 for tag, pos in (("0", y), ("m", ym), ("p", yp), ("2", y2)):
-                    recv(f"{'sr' if j == 0 else 'sq'}{t}{tag}", dr.at[kr(t), 1 - core, xh * 4 + pos])
+                    recv(f"{'sr' if j == 0 else 'sq'}{t}{tag}", dr.at[kr(t), 1 - core, xh * 4 + (pos - z + 4) % 4])
 
     for name in ORDER:
         steps[name]()
@@ -322,7 +324,7 @@
     for c in sends.values():
         c.wait_send()
 
-    @pl.when(off_diag)
+    @pl.when(moves)
     def _():
         for t in range(2):
             make(f"sw{t}", dn.at[t], dr.at[kf(t), core, row], d_tr).wait_send()

time: 68.3 us -> 63.2 us (0.925)
  Pallas kernels: 67.2 us -> 62.1 us
    pallas_call x1, Pallas kernels: 61.5 us -> 56.4 us  [local(): pl.pallas_call(exchange_kernel, out_shape=(jax.ShapeDtypeStruct((2, 2, 8,...]
where the time goes in v3:
time: 63.2 us; the launch traced here: 63.1 us
  Pallas kernels  62.1 us (98%)
  local copies, waits for them, and re-layouts  0.93 us (1%)
    pallas_call x1, Pallas kernels, local(): pl.pallas_call(exchange_kernel, out_shape=(jax.ShapeDtypeStruct((2, 2, 8,...  56.4 us
    pallas_call x1, Pallas kernels, local(): pl.pallas_call(outer_kernel, out_shape=jax.ShapeDtypeStruct((2048, 1024),...  5.69 us

profile of v3, /device:TPU:1, one launch (start us, length us, event | category | flops | bytes accessed | tf_op | source)
XLA Modules:
  0.0 63.1 jit_solution(385660908522621501)
XLA Ops:
  0.0 0.0 copy-start.4
  0.0 0.0 copy-start
  0.0 0.9 %copy-done = f32[2048,16]{0,1:T(8,128)S(1)} copy-done((f32[2048,16]{0,1:T(8,128)S(1)}, f32[2048,16]{0,1:T(8,128)}, u32[]{:S(2)}) %copy-start) | copy-done | bytes 131096
  0.9 0.0 copy-start.1
  0.9 0.0 copy-start.2
  0.9 0.0 copy-start.3
  0.9 56.4 %exchange.1 = (f32[2,2,8,128,128]{4,3,2,1,0:T(8,128)S(1)}, f32[2,8,128,128]{3,2,1,0:T(8,128)S(1)}) custom-call(f32[2048,1024]{1,0:T(8,128)} %a_hbm.1, f32[16,2048]{1,0:T(8,128)S(1)} %bitcast.6), custom_call_target="tpu_custom_call" | custom-call | tf_op jit(solution)/shard_map/exchange/pallas_call | solution.py:390
  57.4 0.0 copy-done.4
  57.4 0.0 copy-done.1
  57.4 0.0 copy-done.2
  57.4 0.0 copy-done.3
  57.4 5.7 %outer.1 = f32[2048,1024]{1,0:T(8,128)} custom-call(f32[2,2048,128]{2,1,0:T(8,128)S(1)} %bitcast.5, f32[2,8,128,128]{3,2,1,0:T(8,128)S(1)} %get-tuple-element.8.dc_ref, s32[128,128]{1,0:T(8,128)S(1)} %bitcast.7, s32[128,128]{1,0:T(8,128)S(1)} %bitcast.8, f32[16,128]{1,0:T(8,128)S(1)} %bitcast.9, f32[64]{0:T(128)S(1)} %copy-done.4), custom_call_target="tpu_custom_call" | custom-call | tf_op jit(solution)/shard_map/outer/pallas_call | solution.py:424
Async XLA Ops:
  0.0 57.4 %copy-start.4 = (f32[64]{0:T(128)S(1)}, f32[64]{0:T(128)}, u32[]{:S(2)}) copy-start(f32[64]{0:T(128)} %eocc_ref.1) | copy-start | bytes 772
  0.0 0.9 %copy-start = (f32[2048,16]{0,1:T(8,128)S(1)}, f32[2048,16]{0,1:T(8,128)}, u32[]{:S(2)}) copy-start(f32[2048,16]{0,1:T(8,128)} %param.7) | copy-start | bytes 393220
  0.9 56.5 %copy-start.1 = (s32[16384]{0:T(1024)S(1)}, s32[16384]{0:T(1024)}, u32[]{:S(2)}) copy-start(s32[16384]{0:T(1024)} %param.8) | copy-start | bytes 196612
  0.9 56.5 %copy-start.2 = (s32[16384]{0:T(1024)S(1)}, s32[16384]{0:T(1024)}, u32[]{:S(2)}) copy-start(s32[16384]{0:T(1024)} %param.9) | copy-start | bytes 196612
  0.9 56.5 %copy-start.3 = (f32[2048]{0:T(1024)S(1)}, f32[2048]{0:T(1024)}, u32[]{:S(2)}) copy-start(f32[2048]{0:T(1024)} %param.11) | copy-start | bytes 24580

commit v4 on v3

--- a/solution.py
+++ b/solution.py
@@ -11,10 +11,10 @@
 F32 = jnp.float32
 BF16 = jnp.bfloat16
 RING = ("pA", "mB", "pB", "mA", "fA", "fB")
-NAMES = ["fx"]
+NAMES = ["fx", "fy"]
 for t_ in range(2):
     for r_ in ("f0", "f1"):
-        NAMES += [f"{r_}{m_}" for m_ in RING if t_ == 0]
+        NAMES += [f"{r_}{m_}" for m_ in RING if t_ == 0 and (r_ == "f0" or m_[0] != "f")]
     for r_ in ("c0", "c1", "r0", "r1"):
         NAMES += [f"{r_}{t_}{m_}" for m_ in RING]
     NAMES += [f"{q_}{t_}{j_}" for q_ in ("sf", "sr", "sq") for j_ in ("0", "m", "p", "2")]
@@ -22,14 +22,13 @@
 ID = {n_: i_ for i_, n_ in enumerate(NAMES)}
 
 ORDER = (
-    "f0.own", "spA0", "spA1", "spA2", "spA3", "f0.fA", "f0.fB", "f0.nm", "f0.np", "f1.own", "f0.far", "spF0",
-    "mm0.2", "mm0.p", "f1.fA", "f1.fB", "mm0.m", "mm0.0", "f1.nm", "f1.np", "rl0p", "rl0m", "f1.far", "spF1",
-    "mm1.2", "mm1.p", "mm1.m", "mm1.0", "cr0", "rl1p", "rl1m", "c00.own", "cr1", "c10.own", "c00.fA", "c00.fB",
-    "c01.own", "r00.own", "c00.nm", "c00.np", "c10.fA", "c10.fB", "r10.own", "c10.nm", "c10.np", "c00.far",
-    "c11.own", "r00.fA", "r00.fB", "c01.fA", "c01.fB", "r00.nm", "r00.np", "c01.nm", "c01.np", "r01.own",
-    "r10.fA", "r10.fB", "c10.far", "r10.nm", "r10.np", "r11.own", "c11.fA", "c11.fB", "r00.far", "c11.nm",
-    "c11.np", "r01.fA", "r01.fB", "c01.far", "r01.nm", "r01.np", "c11.far", "r10.far", "r11.fA", "r11.fB",
-    "rf0", "r11.nm", "r11.np", "r01.far", "r11.far", "rf1",
+    "f0.own", "spA", "f0.fA", "f0.fB", "f0.nm", "f0.np", "f1.own", "f0.far", "spF0", "mm0", "f1.nm", "f1.np",
+    "f1.far", "rl0p", "rl0m", "spF1", "mm1", "cr0", "rl1p", "rl1m", "c00.own", "cr1", "c10.own", "c00.fA",
+    "c00.fB", "c00.nm", "c01.own", "c00.np", "r00.own", "c10.fA", "c10.fB", "c10.nm", "c10.np", "c00.far",
+    "c11.own", "r00.fA", "r00.fB", "c01.fA", "c01.fB", "r01.own", "r10.own", "r00.nm", "r00.np", "c01.nm",
+    "c01.np", "c10.far", "r11.own", "r00.far", "c11.fA", "c11.fB", "r01.fA", "r01.fB", "c11.nm", "c11.np",
+    "r01.nm", "r01.np", "c01.far", "r10.fA", "r10.fB", "c11.far", "r10.nm", "r10.np", "r11.fA", "r11.fB",
+    "r11.nm", "r11.np", "r01.far", "r10.far", "r11.far", "rf0", "rf1",
 )
 
 
@@ -90,7 +89,7 @@
             steps[name] = f
         return keep
 
-    def ring(n, slot, pos, to_up, to_down, half, own, sib=None):
+    def ring(n, slot, pos, to_up, to_down, half, own, sib=None, far=None):
         u, d, o = (pos + 1) % 4, (pos + 3) % 4, (pos + 2) % 4
 
         def part(i, which):
@@ -111,15 +110,16 @@
         def _():
             own(send_own)
 
-        @step(n + ".fA")
-        def _():
-            recv(n + "pA", part(d, 0))
-            start(n + "fA", part(d, 0), part(d, 0), to_up)
-
-        @step(n + ".fB")
-        def _():
-            recv(n + "mB", part(u, 1))
-            start(n + "fB", part(u, 1), part(u, 1), to_down)
+        if far is None:
+            @step(n + ".fA")
+            def _():
+                recv(n + "pA", part(d, 0))
+                start(n + "fA", part(d, 0), part(d, 0), to_up)
+
+            @step(n + ".fB")
+            def _():
+                recv(n + "mB", part(u, 1))
+                start(n + "fB", part(u, 1), part(u, 1), to_down)
 
         @step(n + ".nm")
         def _():
@@ -135,8 +135,13 @@
 
         @step(n + ".far")
         def _():
-            recv(n + "fA", part(o, 0))
-            recv(n + "fB", part(o, 1))
+            if far is None:
+                recv(n + "fA", part(o, 0))
+                recv(n + "fB", part(o, 1))
+            else:
+                recv(far, slot(o))
+            if n == "f0":
+                start("fy", slot(o), slot(o), d_x2)
             to_sib("2", o)
 
     def a_copy(i):
@@ -176,22 +181,22 @@
         send()
 
     for t, own in enumerate((own_f0, own_f1)):
-        ring(f"f{t}", lambda i, t=t: ft.at[kf(t), i, core], y, d_yp, d_ym, 8, own, f"sf{t}")
-
-    for q in range(4):
-        @step(f"spA{q}")
-        def _(q=q):
-            def body(i, carry):
-                a_copy(i).wait()
-                rows = pl.ds(pl.multiple_of(i * 256, 256), 256)
-                for xl in range(2):
-                    for zz in range(4):
-                        r = xl * 4 + zz
-                        h, l = split(abuf[rows, r * 128:(r + 1) * 128])
-                        ah[zz, rows, xl * 128:(xl + 1) * 128] = h
-                        al[zz, rows, xl * 128:(xl + 1) * 128] = l
-                return carry
-            lax.fori_loop(2 * q, 2 * q + 2, body, 0)
+        ring(f"f{t}", lambda i, t=t: ft.at[kf(t), i, core], y, d_yp, d_ym, 8, own, f"sf{t}",
+             "fy" if t == 1 else None)
+
+    @step("spA")
+    def _():
+        def body(i, carry):
+            a_copy(i).wait()
+            rows = pl.ds(pl.multiple_of(i * 256, 256), 256)
+            for xl in range(2):
+                for zz in range(4):
+                    r = xl * 4 + zz
+                    h, l = split(abuf[rows, r * 128:(r + 1) * 128])
+                    ah[zz, rows, xl * 128:(xl + 1) * 128] = h
+                    al[zz, rows, xl * 128:(xl + 1) * 128] = l
+            return carry
+        lax.fori_loop(0, 8, body, 0)
 
     up, down = pl.ds(0, 64), pl.ds(64, 64)
 
@@ -220,25 +225,36 @@
             fhl[0:128] = hi
             fhl[128:256] = lo
 
-        @step(f"mm{t}.2")
-        def _(t=t):
-            product(t, z2)
-            start(f"s1p{t}", pt.at[t, z2, :, up], r1a.at[t], d_zp)
-            start(f"s1m{t}", pt.at[t, z2, :, down], r1b.at[t], d_zm)
-
-        @step(f"mm{t}.p")
-        def _(t=t):
-            product(t, zp)
-            start(f"s2pB{t}", pt.at[t, zp, :, down], r2p.at[t, :, down], d_zp)
-
-        @step(f"mm{t}.m")
-        def _(t=t):
-            product(t, zm)
-            start(f"s2mA{t}", pt.at[t, zm, :, up], r2m.at[t, :, up], d_zm)
-
-        @step(f"mm{t}.0")
-        def _(t=t):
-            product(t, z)
+        @step(f"mm{t}")
+        def _(t=t):
+            first = [
+                make(f"s1p{t}", pt.at[t, z2, :, up], r1a.at[t], d_zp),
+                make(f"s1m{t}", pt.at[t, z2, :, down], r1b.at[t], d_zm),
+            ]
+            above = make(f"s2pB{t}", pt.at[t, zp, :, down], r2p.at[t, :, down], d_zp)
+            below = make(f"s2mA{t}", pt.at[t, zm, :, up], r2m.at[t, :, up], d_zm)
+            sends.update({f"s1p{t}": first[0], f"s1m{t}": first[1], f"s2pB{t}": above, f"s2mA{t}": below})
+
+            def body(i, carry):
+                zz = jnp.where(i == 0, z2, jnp.where(i == 1, zp, jnp.where(i == 2, zm, z)))
+                product(t, zz)
+
+                @pl.when(i == 0)
+                def _():
+                    first[0].start()
+                    first[1].start()
+
+                @pl.when(i == 1)
+                def _():
+                    above.start()
+
+                @pl.when(i == 2)
+                def _():
+                    below.start()
+
+                return carry
+
+            lax.fori_loop(0, 4, body, 0)
 
         @step(f"rl{t}p")
         def _(t=t):
@@ -267,7 +283,8 @@
             recv(f"s3{t}", r3.at[t])
             d = own + r3[t]
             dn[t] = d.T
-            start(f"sx{t}", dn.at[t], dr.at[kf(t), core, row], d_tx)
+            if t == 1:
+                start(f"sx{t}", dn.at[t], dr.at[kf(t), core, row], d_tx)
 
             @pl.when(moves)
             def _():
@@ -297,6 +314,8 @@
             def _():
                 pltpu.make_async_copy(dn.at[t], mine, msem.at[t]).wait()
 
+            if t == 0:
+                start(f"sx{t}", mine, mine, d_x2)
             send()
 
         def own_r1(send, t=t):

time: 63.2 us -> 61.2 us (0.968)
  Pallas kernels: 62.1 us -> 60.1 us
    pallas_call x1, Pallas kernels: 56.4 us -> 54.4 us  [local(): pl.pallas_call(exchange_kernel, out_shape=(jax.ShapeDtypeStruct((2, 2, 8,...]
where the time goes in v4:
time: 61.2 us; the launch traced here: 61.1 us
  Pallas kernels  60.1 us (98%)
  local copies, waits for them, and re-layouts  0.93 us (2%)
    pallas_call x1, Pallas kernels, local(): pl.pallas_call(exchange_kernel, out_shape=(jax.ShapeDtypeStruct((2, 2, 8,...  54.4 us
    pallas_call x1, Pallas kernels, local(): pl.pallas_call(outer_kernel, out_shape=jax.ShapeDtypeStruct((2048, 1024),...  5.7 us

profile of v4, /device:TPU:1, one launch (start us, length us, event | category | flops | bytes accessed | tf_op | source)
XLA Modules:
  0.0 61.1 jit_solution(9807046920431522136)
XLA Ops:
  0.0 0.0 copy-start.4
  0.0 0.0 copy-start
  0.0 0.9 %copy-done = f32[2048,16]{0,1:T(8,128)S(1)} copy-done((f32[2048,16]{0,1:T(8,128)S(1)}, f32[2048,16]{0,1:T(8,128)}, u32[]{:S(2)}) %copy-start) | copy-done | bytes 131096
  0.9 0.0 copy-start.1
  0.9 0.0 copy-start.2
  0.9 0.0 copy-start.3
  0.9 54.4 %exchange.1 = (f32[2,2,8,128,128]{4,3,2,1,0:T(8,128)S(1)}, f32[2,8,128,128]{3,2,1,0:T(8,128)S(1)}) custom-call(f32[2048,1024]{1,0:T(8,128)} %a_hbm.1, f32[16,2048]{1,0:T(8,128)S(1)} %bitcast.6), custom_call_target="tpu_custom_call" | custom-call | tf_op jit(solution)/shard_map/exchange/pallas_call | solution.py:409
  55.4 0.0 copy-done.4
  55.4 0.0 copy-done.1
  55.4 0.0 copy-done.2
  55.4 0.0 copy-done.3
  55.4 5.7 %outer.1 = f32[2048,1024]{1,0:T(8,128)} custom-call(f32[2,2048,128]{2,1,0:T(8,128)S(1)} %bitcast.5, f32[2,8,128,128]{3,2,1,0:T(8,128)S(1)} %get-tuple-element.8.dc_ref, s32[128,128]{1,0:T(8,128)S(1)} %bitcast.7, s32[128,128]{1,0:T(8,128)S(1)} %bitcast.8, f32[16,128]{1,0:T(8,128)S(1)} %bitcast.9, f32[64]{0:T(128)S(1)} %copy-done.4), custom_call_target="tpu_custom_call" | custom-call | tf_op jit(solution)/shard_map/outer/pallas_call | solution.py:443
Async XLA Ops:
  0.0 55.4 %copy-start.4 = (f32[64]{0:T(128)S(1)}, f32[64]{0:T(128)}, u32[]{:S(2)}) copy-start(f32[64]{0:T(128)} %eocc_ref.1) | copy-start | bytes 772
  0.0 0.9 %copy-start = (f32[2048,16]{0,1:T(8,128)S(1)}, f32[2048,16]{0,1:T(8,128)}, u32[]{:S(2)}) copy-start(f32[2048,16]{0,1:T(8,128)} %param.7) | copy-start | bytes 393220
  0.9 54.4 %copy-start.1 = (s32[16384]{0:T(1024)S(1)}, s32[16384]{0:T(1024)}, u32[]{:S(2)}) copy-start(s32[16384]{0:T(1024)} %param.8) | copy-start | bytes 196612
  0.9 54.4 %copy-start.2 = (s32[16384]{0:T(1024)S(1)}, s32[16384]{0:T(1024)}, u32[]{:S(2)}) copy-start(s32[16384]{0:T(1024)} %param.9) | copy-start | bytes 196612
  0.9 54.5 %copy-start.3 = (f32[2048]{0:T(1024)S(1)}, f32[2048]{0:T(1024)}, u32[]{:S(2)}) copy-start(f32[2048]{0:T(1024)} %param.11) | copy-start | bytes 24580

commit v5 on v4

--- a/solution.py
+++ b/solution.py
@@ -18,17 +18,17 @@
     for r_ in ("c0", "c1", "r0", "r1"):
         NAMES += [f"{r_}{t_}{m_}" for m_ in RING]
     NAMES += [f"{q_}{t_}{j_}" for q_ in ("sf", "sr", "sq") for j_ in ("0", "m", "p", "2")]
-    NAMES += [f"{m_}{t_}" for m_ in ("s1p", "s1m", "s2pA", "s2pB", "s2mA", "s2mB", "s3", "cx", "sw", "sx")]
+    NAMES += [f"{m_}{t_}" for m_ in ("p0", "p1", "p2", "p3", "p4", "p5", "p6", "cx", "sw", "sx")]
 ID = {n_: i_ for i_, n_ in enumerate(NAMES)}
 
 ORDER = (
     "f0.own", "spA", "f0.fA", "f0.fB", "f0.nm", "f0.np", "f1.own", "f0.far", "spF0", "mm0", "f1.nm", "f1.np",
-    "f1.far", "rl0p", "rl0m", "spF1", "mm1", "cr0", "rl1p", "rl1m", "c00.own", "cr1", "c10.own", "c00.fA",
-    "c00.fB", "c00.nm", "c01.own", "c00.np", "r00.own", "c10.fA", "c10.fB", "c10.nm", "c10.np", "c00.far",
-    "c11.own", "r00.fA", "r00.fB", "c01.fA", "c01.fB", "r01.own", "r10.own", "r00.nm", "r00.np", "c01.nm",
-    "c01.np", "c10.far", "r11.own", "r00.far", "c11.fA", "c11.fB", "r01.fA", "r01.fB", "c11.nm", "c11.np",
-    "r01.nm", "r01.np", "c01.far", "r10.fA", "r10.fB", "c11.far", "r10.nm", "r10.np", "r11.fA", "r11.fB",
-    "r11.nm", "r11.np", "r01.far", "r10.far", "r11.far", "rf0", "rf1",
+    "f1.far", "spF1", "mm1", "c00.own", "c01.own", "c10.own", "c00.fA", "c00.fB", "c00.nm", "c00.np",
+    "r00.own", "c11.own", "r00.fA", "r00.fB", "r01.own", "c01.fA", "c01.fB", "r00.nm", "r00.np", "c01.nm",
+    "c01.np", "r10.own", "c10.fA", "c10.fB", "r11.own", "c10.nm", "c10.np", "r00.far", "c00.far", "r01.fA",
+    "r01.fB", "c11.fA", "c11.fB", "r01.nm", "r01.np", "c11.nm", "c11.np", "r10.fA", "r10.fB", "c01.far",
+    "r10.nm", "r10.np", "c10.far", "r11.fA", "r11.fB", "c11.far", "r11.nm", "r11.np", "r01.far", "r10.far",
+    "r11.far", "rf0", "rf1",
 )
 
 
@@ -39,7 +39,7 @@
 
 def exchange_kernel(
     a_hbm, f_hbm, dr, dc,
-    abuf, ah, al, ft, fhl, pt, r1a, r1b, r2p, r2m, sx, r3, dp, dn,
+    abuf, ah, al, ft, fhl, pt, rb, dp, dn,
     ssem, rsem, asem, lsem, msem,
 ):
     row, col = lax.axis_index("row"), lax.axis_index("col")
@@ -58,9 +58,7 @@
     d_xn = dev(x_hi, 1 - x_lo, y, z, core)
     d_sib = dev(x_hi, x_lo, y, z, 1 - core)
     d_tr = dev(x_lo, x_hi, (y + z) % 4, y, core)
-    d_from_tr = dev(x_lo, x_hi, z, (y - z + 4) % 4, core)
     d_tx = dev(1 - x_lo, x_hi, (y + z) % 4, y, core)
-    d_from_tx = dev(x_lo, 1 - x_hi, z, (y - z + 4) % 4, core)
     stays = (x_hi == x_lo) & (y == 0) & (z == 0)
     moves = jnp.logical_not(stays)
     diag = row == s
@@ -154,17 +152,11 @@
     own_f.start()
 
     barrier = pltpu.get_barrier_semaphore()
-    for d in (d_yp, d_ym, d_zp, d_zm, d_x2, d_xn, d_sib, d_from_tx):
+    group = [dev(x_hi, xl, y, zz, core) for xl in (x_lo, 1 - x_lo) for zz in (z, zp, zm, z2)][1:]
+    greeted = [d_yp, d_ym, d_x2, d_sib] + group
+    for d in greeted:
         pl.semaphore_signal(barrier, inc=1, device_id=d, device_id_type=MESH)
-
-    @pl.when(moves)
-    def _():
-        pl.semaphore_signal(barrier, inc=1, device_id=d_from_tr, device_id_type=MESH)
-        pl.semaphore_wait(barrier, 9)
-
-    @pl.when(stays)
-    def _():
-        pl.semaphore_wait(barrier, 8)
+    pl.semaphore_wait(barrier, len(greeted))
 
     def kf(t):
         return x_hi if t == 0 else 1 - x_hi
@@ -198,7 +190,7 @@
             return carry
         lax.fori_loop(0, 8, body, 0)
 
-    up, down = pl.ds(0, 64), pl.ds(64, 64)
+    targets = [(xl, zz) for zz in (z2, zp, zm) for xl in (x_lo, 1 - x_lo)] + [(1 - x_lo, z)]
 
     def product(t, zz):
         h = kf(t)
@@ -227,61 +219,30 @@
 
         @step(f"mm{t}")
         def _(t=t):
-            first = [
-                make(f"s1p{t}", pt.at[t, z2, :, up], r1a.at[t], d_zp),
-                make(f"s1m{t}", pt.at[t, z2, :, down], r1b.at[t], d_zm),
-            ]
-            above = make(f"s2pB{t}", pt.at[t, zp, :, down], r2p.at[t, :, down], d_zp)
-            below = make(f"s2mA{t}", pt.at[t, zm, :, up], r2m.at[t, :, up], d_zm)
-            sends.update({f"s1p{t}": first[0], f"s1m{t}": first[1], f"s2pB{t}": above, f"s2mA{t}": below})
+            pairs = []
+            for k, (xl, zz) in enumerate(targets):
+                pairs.append(make(f"p{k}{t}", pt.at[t, zz, xl], rb.at[t, k], dev(x_hi, xl, y, zz, core)))
+                sends[f"p{k}{t}"] = pairs[-1]
 
             def body(i, carry):
                 zz = jnp.where(i == 0, z2, jnp.where(i == 1, zp, jnp.where(i == 2, zm, z)))
                 product(t, zz)
 
-                @pl.when(i == 0)
-                def _():
-                    first[0].start()
-                    first[1].start()
-
-                @pl.when(i == 1)
-                def _():
-                    above.start()
-
-                @pl.when(i == 2)
-                def _():
-                    below.start()
+                for j in range(4):
+                    @pl.when(i == j)
+                    def _(j=j):
+                        for c in pairs[2 * j:2 * j + 2]:
+                            c.start()
 
                 return carry
 
             lax.fori_loop(0, 4, body, 0)
 
-        @step(f"rl{t}p")
-        def _(t=t):
-            recv(f"s1p{t}", r1a.at[t])
-            pt[t, zp, :, 0:64] += r1a[t]
-            start(f"s2pA{t}", pt.at[t, zp, :, up], r2p.at[t, :, up], d_zp)
-
-        @step(f"rl{t}m")
-        def _(t=t):
-            recv(f"s1m{t}", r1b.at[t])
-            pt[t, zm, :, 64:128] += r1b[t]
-            start(f"s2mB{t}", pt.at[t, zm, :, down], r2m.at[t, :, down], d_zm)
-
-        @step(f"cr{t}")
-        def _(t=t):
-            recv(f"s2pA{t}", r2p.at[t, :, up])
-            recv(f"s2pB{t}", r2p.at[t, :, down])
-            recv(f"s2mA{t}", r2m.at[t, :, up])
-            recv(f"s2mB{t}", r2m.at[t, :, down])
-            o = 1 - x_lo
-            sx[t] = pt[t, z, o] + r2p[t, o] + r2m[t, o]
-            start(f"s3{t}", sx.at[t], r3.at[t], d_xn)
-
         def own_c0(send, t=t):
-            own = pt[t, z, x_lo] + r2p[t, x_lo] + r2m[t, x_lo]
-            recv(f"s3{t}", r3.at[t])
-            d = own + r3[t]
+            d = pt[t, z, x_lo]
+            for k in range(7):
+                recv(f"p{k}{t}", rb.at[t, k])
+                d = d + rb[t, k]
             dn[t] = d.T
             if t == 1:
                 start(f"sx{t}", dn.at[t], dr.at[kf(t), core, row], d_tx)
@@ -421,12 +382,7 @@
             vmem(2, 4, 2, 16, 2048),
             pltpu.VMEM((256, 2048), BF16),
             vmem(2, 4, 2, 128, 128),
-            vmem(2, 2, 64, 128),
-            vmem(2, 2, 64, 128),
-            vmem(2, 2, 128, 128),
-            vmem(2, 2, 128, 128),
-            vmem(2, 128, 128),
-            vmem(2, 128, 128),
+            vmem(2, 7, 128, 128),
             vmem(2, 128, 128),
             vmem(2, 128, 128),
             pltpu.SemaphoreType.DMA((len(NAMES),)),
@@ -438,7 +394,7 @@
         compiler_params=pltpu.CompilerParams(
             collective_id=0, has_side_effects=True, vmem_limit_bytes=48 * 1024 * 1024),
         name="exchange",
-    )(amplitudes, factors.T)
+    )(amplitudes, pltpu.with_memory_space_constraint(factors.T, pltpu.HBM))
     in_vmem = pl.BlockSpec(memory_space=pltpu.VMEM)
     return pl.pallas_call(
         outer_kernel,

time: 61.2 us -> 57.9 us (0.946)
  Pallas kernels: 60.1 us -> 57.8 us
  local copies, waits for them, and re-layouts: 0.93 us -> 0.02 us
    pallas_call x1, Pallas kernels: 54.4 us -> 52.1 us  [local(): pl.pallas_call(exchange_kernel, out_shape=(jax.ShapeDtypeStruct((2, 2, 8,...]
    unnamed x10 -> x8, local copies, waits for them, and re-layouts: 0.93 us -> 0.02 us
where the time goes in v5:
time: 57.9 us; the launch traced here: 57.8 us
  Pallas kernels  57.8 us (100%)
    pallas_call x1, Pallas kernels, local(): pl.pallas_call(exchange_kernel, out_shape=(jax.ShapeDtypeStruct((2, 2, 8,...  52.1 us
    pallas_call x1, Pallas kernels, local(): pl.pallas_call(outer_kernel, out_shape=jax.ShapeDtypeStruct((2048, 1024),...  5.69 us

profile of v5, /device:TPU:1, one launch (start us, length us, event | category | flops | bytes accessed | tf_op | source)
XLA Modules:
  0.0 57.8 jit_solution(5177145598309761466)
XLA Ops:
  0.0 0.0 copy-start.2
  0.0 0.0 copy-start.3
  0.0 0.0 copy-start.1
  0.0 0.0 copy-start
  0.0 52.1 %exchange.1 = (f32[2,2,8,128,128]{4,3,2,1,0:T(8,128)S(1)}, f32[2,8,128,128]{3,2,1,0:T(8,128)S(1)}) custom-call(f32[2048,1024]{1,0:T(8,128)} %a_hbm.1, f32[16,2048]{1,0:T(8,128)} %bitcast.9), custom_call_target="tpu_custom_call" | custom-call | tf_op jit(solution)/shard_map/exchange/pallas_call | solution.py:370
  52.1 0.0 copy-done.2
  52.1 0.0 copy-done.3
  52.1 0.0 copy-done.1
  52.1 0.0 copy-done
  52.1 5.7 %outer.1 = f32[2048,1024]{1,0:T(8,128)} custom-call(f32[2,2048,128]{2,1,0:T(8,128)S(1)} %bitcast.5, f32[2,8,128,128]{3,2,1,0:T(8,128)S(1)} %get-tuple-element.8.dc_ref, s32[128,128]{1,0:T(8,128)S(1)} %bitcast.6, s32[128,128]{1,0:T(8,128)S(1)} %bitcast.7, f32[16,128]{1,0:T(8,128)S(1)} %bitcast.8, f32[64]{0:T(128)S(1)} %copy-done.3), custom_call_target="tpu_custom_call" | custom-call | tf_op jit(solution)/shard_map/outer/pallas_call | solution.py:399
Async XLA Ops:
  0.0 52.1 %copy-start.2 = (f32[2048]{0:T(1024)S(1)}, f32[2048]{0:T(1024)}, u32[]{:S(2)}) copy-start(f32[2048]{0:T(1024)} %param.11) | copy-start | bytes 24580
  0.0 52.1 %copy-start.3 = (f32[64]{0:T(128)S(1)}, f32[64]{0:T(128)}, u32[]{:S(2)}) copy-start(f32[64]{0:T(128)} %eocc_ref.1) | copy-start | bytes 772
  0.0 52.1 %copy-start.1 = (s32[16384]{0:T(1024)S(1)}, s32[16384]{0:T(1024)}, u32[]{:S(2)}) copy-start(s32[16384]{0:T(1024)} %param.9) | copy-start | bytes 196612
  0.0 52.1 %copy-start = (s32[16384]{0:T(1024)S(1)}, s32[16384]{0:T(1024)}, u32[]{:S(2)}) copy-start(s32[16384]{0:T(1024)} %param.8) | copy-start | bytes 196612

commit v6 on v5

--- a/solution.py
+++ b/solution.py
@@ -22,8 +22,8 @@
 ID = {n_: i_ for i_, n_ in enumerate(NAMES)}
 
 ORDER = (
-    "f0.own", "spA", "f0.fA", "f0.fB", "f0.nm", "f0.np", "f1.own", "f0.far", "spF0", "mm0", "f1.nm", "f1.np",
-    "f1.far", "spF1", "mm1", "c00.own", "c01.own", "c10.own", "c00.fA", "c00.fB", "c00.nm", "c00.np",
+    "f0.own", "spA", "f0.fA", "f0.fB", "f0.nm", "f0.np", "f1.own", "f0.far", "spF0", "mm0a", "f1.nm", "f1.np",
+    "mm0b", "f1.far", "spF1", "mm1", "c00.own", "c01.own", "c10.own", "c00.fA", "c00.fB", "c00.nm", "c00.np",
     "r00.own", "c11.own", "r00.fA", "r00.fB", "r01.own", "c01.fA", "c01.fB", "r00.nm", "r00.np", "c01.nm",
     "c01.np", "r10.own", "c10.fA", "c10.fB", "r11.own", "c10.nm", "c10.np", "r00.far", "c00.far", "r01.fA",
     "r01.fB", "c11.fA", "c11.fB", "r01.nm", "r01.np", "c11.nm", "c11.np", "r10.fA", "r10.fB", "c01.far",
@@ -217,12 +217,16 @@
             fhl[0:128] = hi
             fhl[128:256] = lo
 
-        @step(f"mm{t}")
-        def _(t=t):
-            pairs = []
-            for k, (xl, zz) in enumerate(targets):
-                pairs.append(make(f"p{k}{t}", pt.at[t, zz, xl], rb.at[t, k], dev(x_hi, xl, y, zz, core)))
-                sends[f"p{k}{t}"] = pairs[-1]
+        pairs_of = {}
+
+        def products(t, lo, hi, pairs_of=pairs_of):
+            if lo == 0:
+                pairs_of[t] = []
+                for k, (xl, zz) in enumerate(targets):
+                    to = dev(x_hi, xl, y, zz, core)
+                    pairs_of[t].append(make(f"p{k}{t}", pt.at[t, zz, xl], rb.at[t, k], to))
+                    sends[f"p{k}{t}"] = pairs_of[t][-1]
+            pairs = pairs_of[t]
 
             def body(i, carry):
                 zz = jnp.where(i == 0, z2, jnp.where(i == 1, zp, jnp.where(i == 2, zm, z)))
@@ -236,7 +240,13 @@
 
                 return carry
 
-            lax.fori_loop(0, 4, body, 0)
+            lax.fori_loop(lo, hi, body, 0)
+
+        cuts = (0, 2, 4) if t == 0 else (0, 4)
+        for j in range(len(cuts) - 1):
+            @step(f"mm{t}" + ("ab"[j] if t == 0 else ""))
+            def _(t=t, lo=cuts[j], hi=cuts[j + 1], products=products):
+                products(t, lo, hi)
 
         def own_c0(send, t=t):
             d = pt[t, z, x_lo]
@@ -313,7 +323,7 @@
         pltpu.make_async_copy(dp.at[t], dc.at[kf(t), row], lsem.at[1 + t]).wait()
 
 
-OUTER_ROWS = (128, 384, 512, 512, 512)
+OUTER_ROWS = (512, 512, 512, 384, 128)
 
 
 def outer_kernel(dr_ref, dc_ref, occ_ref, vir_ref, evir_ref, eocc_ref, out_hbm, ch, cl, ecol, erow, obuf, sem):

time: 57.9 us -> 57.6 us (level)
  no operation moved by 1% of the time
where the time goes in v6:
time: 57.6 us; the launch traced here: 57.5 us
  Pallas kernels  57.4 us (100%)
    pallas_call x1, Pallas kernels, local(): pl.pallas_call(exchange_kernel, out_shape=(jax.ShapeDtypeStruct((2, 2, 8,...  52.1 us
    pallas_call x1, Pallas kernels, local(): pl.pallas_call(outer_kernel, out_shape=jax.ShapeDtypeStruct((2048, 1024),...  5.32 us

profile of v6, /device:TPU:1, one launch (start us, length us, event | category | flops | bytes accessed | tf_op | source)
XLA Modules:
  0.0 57.5 jit_solution(99132738683783596)
XLA Ops:
  0.0 0.0 copy-start.2
  0.0 0.0 copy-start.3
  0.0 0.0 copy-start.1
  0.0 0.0 copy-start
  0.0 52.1 %exchange.1 = (f32[2,2,8,128,128]{4,3,2,1,0:T(8,128)S(1)}, f32[2,8,128,128]{3,2,1,0:T(8,128)S(1)}) custom-call(f32[2048,1024]{1,0:T(8,128)} %a_hbm.1, f32[16,2048]{1,0:T(8,128)} %bitcast.9), custom_call_target="tpu_custom_call" | custom-call | tf_op jit(solution)/shard_map/exchange/pallas_call | solution.py:380
  52.1 0.0 copy-done.2
  52.1 0.0 copy-done.3
  52.1 0.0 copy-done.1
  52.1 0.0 copy-done
  52.1 5.3 %outer.1 = f32[2048,1024]{1,0:T(8,128)} custom-call(f32[2,2048,128]{2,1,0:T(8,128)S(1)} %bitcast.5, f32[2,8,128,128]{3,2,1,0:T(8,128)S(1)} %get-tuple-element.8.dc_ref, s32[128,128]{1,0:T(8,128)S(1)} %bitcast.6, s32[128,128]{1,0:T(8,128)S(1)} %bitcast.7, f32[16,128]{1,0:T(8,128)S(1)} %bitcast.8, f32[64]{0:T(128)S(1)} %copy-done.3), custom_call_target="tpu_custom_call" | custom-call | tf_op jit(solution)/shard_map/outer/pallas_call | solution.py:409
Async XLA Ops:
  0.0 52.1 %copy-start.2 = (f32[2048]{0:T(1024)S(1)}, f32[2048]{0:T(1024)}, u32[]{:S(2)}) copy-start(f32[2048]{0:T(1024)} %param.11) | copy-start | bytes 24580
  0.0 52.1 %copy-start.3 = (f32[64]{0:T(128)S(1)}, f32[64]{0:T(128)}, u32[]{:S(2)}) copy-start(f32[64]{0:T(128)} %eocc_ref.1) | copy-start | bytes 772
  0.0 52.1 %copy-start.1 = (s32[16384]{0:T(1024)S(1)}, s32[16384]{0:T(1024)}, u32[]{:S(2)}) copy-start(s32[16384]{0:T(1024)} %param.9) | copy-start | bytes 196612
  0.0 52.1 %copy-start = (s32[16384]{0:T(1024)S(1)}, s32[16384]{0:T(1024)}, u32[]{:S(2)}) copy-start(s32[16384]{0:T(1024)} %param.8) | copy-start | bytes 196612

commit v7 on v6

--- a/solution.py
+++ b/solution.py
@@ -323,7 +323,7 @@
         pltpu.make_async_copy(dp.at[t], dc.at[kf(t), row], lsem.at[1 + t]).wait()
 
 
-OUTER_ROWS = (512, 512, 512, 384, 128)
+OUTER_ROWS = (768, 640, 512, 128)
 
 
 def outer_kernel(dr_ref, dc_ref, occ_ref, vir_ref, evir_ref, eocc_ref, out_hbm, ch, cl, ecol, erow, obuf, sem):

time: 57.6 us -> 57.9 us (level)
  no operation moved by 1% of the time
where the time goes in v7:
time: 57.9 us; the launch traced here: 57.8 us
  Pallas kernels  57.8 us (100%)
    pallas_call x1, Pallas kernels, local(): pl.pallas_call(exchange_kernel, out_shape=(jax.ShapeDtypeStruct((2, 2, 8,...  52.1 us
    pallas_call x1, Pallas kernels, local(): pl.pallas_call(outer_kernel, out_shape=jax.ShapeDtypeStruct((2048, 1024),...  5.7 us

profile of v7, /device:TPU:1, one launch (start us, length us, event | category | flops | bytes accessed | tf_op | source)
XLA Modules:
  0.0 57.8 jit_solution(11392325464731134247)
XLA Ops:
  0.0 0.0 copy-start.2
  0.0 0.0 copy-start.3
  0.0 0.0 copy-start.1
  0.0 0.0 copy-start
  0.0 52.1 %exchange.1 = (f32[2,2,8,128,128]{4,3,2,1,0:T(8,128)S(1)}, f32[2,8,128,128]{3,2,1,0:T(8,128)S(1)}) custom-call(f32[2048,1024]{1,0:T(8,128)} %a_hbm.1, f32[16,2048]{1,0:T(8,128)} %bitcast.9), custom_call_target="tpu_custom_call" | custom-call | tf_op jit(solution)/shard_map/exchange/pallas_call | solution.py:380
  52.1 0.0 copy-done.2
  52.1 0.0 copy-done.3
  52.1 0.0 copy-done.1
  52.1 0.0 copy-done
  52.1 5.7 %outer.1 = f32[2048,1024]{1,0:T(8,128)} custom-call(f32[2,2048,128]{2,1,0:T(8,128)S(1)} %bitcast.5, f32[2,8,128,128]{3,2,1,0:T(8,128)S(1)} %get-tuple-element.8.dc_ref, s32[128,128]{1,0:T(8,128)S(1)} %bitcast.6, s32[128,128]{1,0:T(8,128)S(1)} %bitcast.7, f32[16,128]{1,0:T(8,128)S(1)} %bitcast.8, f32[64]{0:T(128)S(1)} %copy-done.3), custom_call_target="tpu_custom_call" | custom-call | tf_op jit(solution)/shard_map/outer/pallas_call | solution.py:409
Async XLA Ops:
  0.0 52.1 %copy-start.2 = (f32[2048]{0:T(1024)S(1)}, f32[2048]{0:T(1024)}, u32[]{:S(2)}) copy-start(f32[2048]{0:T(1024)} %param.11) | copy-start | bytes 24580
  0.0 52.1 %copy-start.3 = (f32[64]{0:T(128)S(1)}, f32[64]{0:T(128)}, u32[]{:S(2)}) copy-start(f32[64]{0:T(128)} %eocc_ref.1) | copy-start | bytes 772
  0.0 52.1 %copy-start.1 = (s32[16384]{0:T(1024)S(1)}, s32[16384]{0:T(1024)}, u32[]{:S(2)}) copy-start(s32[16384]{0:T(1024)} %param.9) | copy-start | bytes 196612
  0.0 52.1 %copy-start = (s32[16384]{0:T(1024)S(1)}, s32[16384]{0:T(1024)}, u32[]{:S(2)}) copy-start(s32[16384]{0:T(1024)} %param.8) | copy-start | bytes 196612
